TPU v7x, 32 devices: a whole 2x2x4 slice. The times are simulated.
32 devices in a mesh: dp: 8 (over y, x, core), seq: 4 (over z).
Axes of the slice: x: 2, y: 2, z: 4, core: 2. Of those that a mesh axis runs over, the one named last changes fastest.
Arguments:
- hidden_states: bfloat16 [8192, 1024], P(('dp', 'seq')), may hold values from -96 to 96
- cotangent: bfloat16 [8192, 1024], P(('dp', 'seq')), may hold values from -6 to 6
- w_qkv: bfloat16 [1024, 3072], P(('dp', 'seq')), may hold values from -0.1875 to 0.1875
- b_query: bfloat16 [1024], P(('dp', 'seq')), may hold values from -3 to 3
- b_value: bfloat16 [1024], P(('dp', 'seq')), may hold values from -0.29882812 to 0.29882812
- w_out: bfloat16 [1024, 1024], P(('dp', 'seq')), may hold values from -3 to 3
- b_out: bfloat16 [1024], P(('dp', 'seq')), may hold values from -3 to 3
- ln1_gain: bfloat16 [1024], P(('dp', 'seq')), may hold values from 0.099609375 to 1.8984375
- ln1_shift: bfloat16 [1024], P(('dp', 'seq')), may hold values from -2 to 2
- w_up: bfloat16 [1024, 4096], P(('dp', 'seq')), may hold values from -0.1875 to 0.1875
- b_up: bfloat16 [4096], P(('dp', 'seq')), may hold values from -3 to 3
- w_down: bfloat16 [1024, 4096], P(('dp', 'seq')), may hold values from -0.09375 to 0.09375
- b_down: bfloat16 [1024], P(('dp', 'seq')), may hold values from -3 to 3
- ln2_gain: bfloat16 [1024], P(('dp', 'seq')), may hold values from 0.099609375 to 1.8984375
- ln2_shift: bfloat16 [1024], P(('dp', 'seq')), may hold values from -2 to 2
Outputs:
- layer_out: bfloat16 [8192, 1024], P(('dp', 'seq'))
- grad_input: float32 [8192, 1024], P(('dp', 'seq'))
- grad_w_qkv: float32 [1024, 3072], P(('dp', 'seq'))
- grad_b_query: float32 [1024], P(('dp', 'seq'))
- grad_b_value: float32 [1024], P(('dp', 'seq'))
- grad_w_out: float32 [1024, 1024], P(('dp', 'seq'))
- grad_b_out: float32 [1024], P(('dp', 'seq'))
- grad_ln1_gain: float32 [1024], P(('dp', 'seq'))
- grad_ln1_shift: float32 [1024], P(('dp', 'seq'))
- grad_w_up: float32 [1024, 4096], P(('dp', 'seq'))
- grad_b_up: float32 [4096], P(('dp', 'seq'))
- grad_w_down: float32 [1024, 4096], P(('dp', 'seq'))
- grad_b_down: float32 [1024], P(('dp', 'seq'))
- grad_ln2_gain: float32 [1024], P(('dp', 'seq'))
- grad_ln2_shift: float32 [1024], P(('dp', 'seq'))
All inputs are finite; a program needn't handle non-finite values.
Results may differ from a plain program's by a relative error of at most 0.018.
The roundings to bfloat16 on the way count: a program that leaves them out, or rounds other values in their place, can miss the bound.
Values may be sent and summed in bfloat16 or wider, within the bound.
No kernel may reach another device: no remote copies, remote signals or barrier semaphores. Data moves between devices by JAX's collectives and lax.ppermute only.
A program may use at most 192 MiB of HBM per device.

v0:
```python
import math

import jax
import jax.numpy as jnp
from jax import lax
from jax.sharding import PartitionSpec as P

HD = 64


EPS = 1e-12


def layer_norm(residual, gain_vec, shift_vec):
    row_mean = jnp.mean(residual, -1, keepdims=True)
    centred = residual - row_mean
    variance = jnp.mean(centred * centred, -1, keepdims=True)
    inv_std = lax.rsqrt(variance + EPS)
    normed = centred * inv_std
    return (normed * gain_vec + shift_vec, normed, inv_std)


def norm_back(incoming, normed, inv_std, gain_vec):
    scaled = incoming * gain_vec
    return inv_std * (
        scaled
        - jnp.mean(scaled, -1, keepdims=True)
        - normed * jnp.mean(scaled * normed, -1, keepdims=True)
    )


def gelu_both(inner):
    normal_cdf = 0.5 * (1.0 + jax.scipy.special.erf(inner / math.sqrt(2.0)))
    gelu_value = inner * normal_cdf
    gelu_slope = normal_cdf + inner * jnp.exp(-0.5 * inner * inner) / math.sqrt(2.0 * math.pi)
    return (gelu_value, gelu_slope)


def contract_last(left, right):
    return lax.dot_general(
        left, right, (((1,), (1,)), ((), ())), preferred_element_type=jnp.float32
    )


def contract_first(left, right):
    return lax.dot_general(
        left, right, (((0,), (0,)), ((), ())), preferred_element_type=jnp.float32
    )


def attend_forward(query_heads, key_heads, value_heads, row_block):
    length, groups_here, head_dim = query_heads.shape
    score_scale = 1.0 / math.sqrt(head_dim)
    blocked = query_heads.reshape(length // row_block, row_block, groups_here, head_dim)

    def one_block(query_block):
        scores = (
            jnp.einsum("qge,kge->gqk", query_block, key_heads, preferred_element_type=jnp.float32)
            * score_scale
        )
        row_max = jnp.max(scores, -1, keepdims=True)
        log_total = row_max + jnp.log(jnp.sum(jnp.exp(scores - row_max), -1, keepdims=True))
        weights = jnp.exp(scores - log_total).astype(jnp.bfloat16)
        outputs = jnp.einsum(
            "gqk,kge->qge", weights, value_heads, preferred_element_type=jnp.float32
        )
        return (outputs.astype(jnp.bfloat16), log_total[:, :, 0])

    outputs, log_total = lax.map(one_block, blocked)
    return (outputs.reshape(length, groups_here, head_dim), log_total)


def attend_backward(query_heads, key_heads, value_heads, outputs, log_total, grad_out, row_block):
    length, groups_here, head_dim = query_heads.shape
    score_scale = 1.0 / math.sqrt(head_dim)
    count_blocks = length // row_block
    row_delta = jnp.sum(grad_out.astype(jnp.float32) * outputs.astype(jnp.float32), -1)

    def blocks_of(tensor):
        return tensor.reshape((count_blocks, row_block) + tensor.shape[1:])

    def one_step(carried, pieces):
        grad_keys, grad_values = carried
        query_block, grad_block, total_block, delta_block = pieces
        scores = (
            jnp.einsum("qge,kge->gqk", query_block, key_heads, preferred_element_type=jnp.float32)
            * score_scale
        )
        probs = jnp.exp(scores - total_block[:, :, None])
        grad_values = grad_values + jnp.einsum(
            "gqk,qge->kge",
            probs.astype(jnp.bfloat16),
            grad_block,
            preferred_element_type=jnp.float32,
        )
        grad_probs = jnp.einsum(
            "qge,kge->gqk", grad_block, value_heads, preferred_element_type=jnp.float32
        )
        grad_scores = (probs * (grad_probs - jnp.transpose(delta_block)[:, :, None])).astype(
            jnp.bfloat16
        )
        grad_query = (
            jnp.einsum("gqk,kge->qge", grad_scores, key_heads, preferred_element_type=jnp.float32)
            * score_scale
        )
        grad_keys = (
            grad_keys
            + jnp.einsum(
                "gqk,qge->kge", grad_scores, query_block, preferred_element_type=jnp.float32
            )
            * score_scale
        )
        return ((grad_keys, grad_values), grad_query.astype(jnp.bfloat16))

    zeros_init = jnp.zeros((length, groups_here, head_dim), jnp.float32)
    (grad_keys, grad_values), grad_query = lax.scan(
        one_step,
        (zeros_init, zeros_init),
        (blocks_of(query_heads), blocks_of(grad_out), log_total, blocks_of(row_delta)),
    )
    return (
        grad_query.reshape(length, groups_here, head_dim),
        grad_keys.astype(jnp.bfloat16),
        grad_values.astype(jnp.bfloat16),
    )


def on_device(
    hidden_states,
    cotangent,
    w_qkv,
    b_query,
    b_value,
    w_out,
    b_out,
    ln1_gain,
    ln1_shift,
    w_up,
    b_up,
    w_down,
    b_down,
    ln2_gain,
    ln2_shift,
):
    (
        full_qkv,
        full_out,
        full_up,
        full_down,
        bias_query,
        bias_value,
        bias_out,
        gain_one,
        shift_one,
        bias_up,
        bias_down,
        gain_two,
        shift_two,
    ) = (
        lax.all_gather(w_qkv, ("dp", "seq"), axis=0, tiled=True),
        lax.all_gather(w_out, ("dp", "seq"), axis=0, tiled=True),
        lax.all_gather(w_up, ("dp", "seq"), axis=0, tiled=True),
        lax.all_gather(w_down, ("dp", "seq"), axis=0, tiled=True),
        lax.all_gather(b_query, ("dp", "seq"), axis=0, tiled=True),
        lax.all_gather(b_value, ("dp", "seq"), axis=0, tiled=True),
        lax.all_gather(b_out, ("dp", "seq"), axis=0, tiled=True),
        lax.all_gather(ln1_gain, ("dp", "seq"), axis=0, tiled=True),
        lax.all_gather(ln1_shift, ("dp", "seq"), axis=0, tiled=True),
        lax.all_gather(b_up, ("dp", "seq"), axis=0, tiled=True),
        lax.all_gather(b_down, ("dp", "seq"), axis=0, tiled=True),
        lax.all_gather(ln2_gain, ("dp", "seq"), axis=0, tiled=True),
        lax.all_gather(ln2_shift, ("dp", "seq"), axis=0, tiled=True),
    )
    model_width = full_out.shape[0]
    bias_front = jnp.concatenate(
        [
            bias_query.astype(jnp.float32),
            jnp.zeros((model_width,), jnp.float32),
            bias_value.astype(jnp.float32),
        ]
    )
    projected = (
        jnp.dot(hidden_states, full_qkv, preferred_element_type=jnp.float32) + bias_front
    ).astype(jnp.bfloat16)
    query_cols, key_cols, value_cols = (
        lax.all_to_all(projected[:, :model_width], "seq", split_axis=1, concat_axis=0, tiled=True),
        lax.all_to_all(
            projected[:, model_width : 2 * model_width],
            "seq",
            split_axis=1,
            concat_axis=0,
            tiled=True,
        ),
        lax.all_to_all(
            projected[:, 2 * model_width :], "seq", split_axis=1, concat_axis=0, tiled=True
        ),
    )
    length = query_cols.shape[0]
    group_cols = query_cols.shape[1]
    groups_here = group_cols // HD
    row_block = min(512, length)

    def heads_of(tensor):
        return tensor.reshape(length, groups_here, HD)

    query_heads = heads_of(query_cols)
    key_heads = heads_of(key_cols)
    value_heads = heads_of(value_cols)
    outputs, log_total = attend_forward(query_heads, key_heads, value_heads, row_block)
    attn_tok = lax.all_to_all(
        outputs.reshape(length, group_cols), "seq", split_axis=0, concat_axis=1, tiled=True
    )
    resid_one = (
        hidden_states.astype(jnp.float32)
        + jnp.dot(attn_tok, full_out, preferred_element_type=jnp.float32)
        + bias_out.astype(jnp.float32)
    )
    hidden_one, normed_one, inv_one = layer_norm(
        resid_one, gain_one.astype(jnp.float32), shift_one.astype(jnp.float32)
    )
    hidden_low = hidden_one.astype(jnp.bfloat16)
    inner = jnp.dot(hidden_low, full_up, preferred_element_type=jnp.float32) + bias_up.astype(
        jnp.float32
    )
    gelu_value, gelu_slope = gelu_both(inner)
    active_low = gelu_value.astype(jnp.bfloat16)
    resid_two = hidden_one + contract_last(active_low, full_down) + bias_down.astype(jnp.float32)
    layer_val, normed_two, inv_two = layer_norm(
        resid_two, gain_two.astype(jnp.float32), shift_two.astype(jnp.float32)
    )
    layer_out = layer_val.astype(jnp.bfloat16)
    back_qkv, back_out, back_up, back_down, back_gain_one, back_gain_two = (
        full_qkv,
        full_out,
        full_up,
        full_down,
        gain_one,
        gain_two,
    )
    grad_y = cotangent.astype(jnp.float32)
    grad_gain_two = jnp.sum(grad_y * normed_two, 0)
    grad_shift_two = jnp.sum(grad_y, 0)
    grad_resid_two = norm_back(grad_y, normed_two, inv_two, back_gain_two.astype(jnp.float32))
    grad_low_two = grad_resid_two.astype(jnp.bfloat16)
    grad_bias_down = jnp.sum(grad_resid_two, 0)
    grad_inner = jnp.dot(grad_low_two, back_down, preferred_element_type=jnp.float32) * gelu_slope
    grad_inner_low = grad_inner.astype(jnp.bfloat16)
    grad_bias_up = jnp.sum(grad_inner, 0)
    grad_hidden = grad_resid_two + contract_last(grad_inner_low, back_up)
    grad_gain_one = jnp.sum(grad_hidden * normed_one, 0)
    grad_shift_one = jnp.sum(grad_hidden, 0)
    grad_resid_one = norm_back(grad_hidden, normed_one, inv_one, back_gain_one.astype(jnp.float32))
    grad_low_one = grad_resid_one.astype(jnp.bfloat16)
    grad_bias_out = jnp.sum(grad_resid_one, 0)
    grad_attn = contract_last(grad_low_one, back_out).astype(jnp.bfloat16)
    grad_attn_cols = lax.all_to_all(grad_attn, "seq", split_axis=1, concat_axis=0, tiled=True)
    grad_query, grad_keys, grad_values = attend_backward(
        query_heads, key_heads, value_heads, outputs, log_total, heads_of(grad_attn_cols), row_block
    )
    grad_query_tok, grad_key_tok, grad_value_tok = (
        lax.all_to_all(
            grad_query.reshape(length, group_cols), "seq", split_axis=0, concat_axis=1, tiled=True
        ),
        lax.all_to_all(
            grad_keys.reshape(length, group_cols), "seq", split_axis=0, concat_axis=1, tiled=True
        ),
        lax.all_to_all(
            grad_values.reshape(length, group_cols), "seq", split_axis=0, concat_axis=1, tiled=True
        ),
    )
    grad_bias_query = jnp.sum(grad_query_tok.astype(jnp.float32), 0)
    grad_bias_value = jnp.sum(grad_value_tok.astype(jnp.float32), 0)
    grad_projected = jnp.concatenate([grad_query_tok, grad_key_tok, grad_value_tok], 1)
    grad_input = grad_resid_one + contract_last(grad_projected, back_qkv)
    left_in, left_attn, left_hidden, left_grad_two = (
        lax.all_gather(hidden_states, "seq", axis=0, tiled=True),
        lax.all_gather(attn_tok, "seq", axis=0, tiled=True),
        lax.all_gather(hidden_low, "seq", axis=0, tiled=True),
        lax.all_gather(grad_low_two, "seq", axis=0, tiled=True),
    )
    right_proj, right_one, right_inner, right_active = (
        lax.all_to_all(grad_projected, "seq", split_axis=1, concat_axis=0, tiled=True),
        lax.all_to_all(grad_low_one, "seq", split_axis=1, concat_axis=0, tiled=True),
        lax.all_to_all(grad_inner_low, "seq", split_axis=1, concat_axis=0, tiled=True),
        lax.all_to_all(active_low, "seq", split_axis=1, concat_axis=0, tiled=True),
    )
    column_terms = (
        contract_first(left_in, right_proj),
        contract_first(left_attn, right_one),
        contract_first(left_hidden, right_inner),
        contract_first(left_grad_two, right_active),
    )
    summed_cols = (
        lax.psum_scatter(
            column_terms[0].astype(jnp.bfloat16), "dp", scatter_dimension=0, tiled=True
        ).astype(jnp.float32),
        lax.psum_scatter(
            column_terms[1].astype(jnp.bfloat16), "dp", scatter_dimension=0, tiled=True
        ).astype(jnp.float32),
        lax.psum_scatter(
            column_terms[2].astype(jnp.bfloat16), "dp", scatter_dimension=0, tiled=True
        ).astype(jnp.float32),
        lax.psum_scatter(
            column_terms[3].astype(jnp.bfloat16), "dp", scatter_dimension=0, tiled=True
        ).astype(jnp.float32),
    )
    sum_qkv, sum_out, sum_up, sum_down = (
        lax.all_to_all(
            summed_cols[0].astype(jnp.bfloat16), "seq", split_axis=0, concat_axis=1, tiled=True
        ).astype(jnp.float32),
        lax.all_to_all(
            summed_cols[1].astype(jnp.bfloat16), "seq", split_axis=0, concat_axis=1, tiled=True
        ).astype(jnp.float32),
        lax.all_to_all(
            summed_cols[2].astype(jnp.bfloat16), "seq", split_axis=0, concat_axis=1, tiled=True
        ).astype(jnp.float32),
        lax.all_to_all(
            summed_cols[3].astype(jnp.bfloat16), "seq", split_axis=0, concat_axis=1, tiled=True
        ).astype(jnp.float32),
    )
    (
        sum_bias_query,
        sum_bias_value,
        sum_bias_out,
        sum_gain_one,
        sum_shift_one,
        sum_bias_up,
        sum_bias_down,
        sum_gain_two,
        sum_shift_two,
    ) = (
        lax.psum_scatter(grad_bias_query, ("dp", "seq"), scatter_dimension=0, tiled=True),
        lax.psum_scatter(grad_bias_value, ("dp", "seq"), scatter_dimension=0, tiled=True),
        lax.psum_scatter(grad_bias_out, ("dp", "seq"), scatter_dimension=0, tiled=True),
        lax.psum_scatter(grad_gain_one, ("dp", "seq"), scatter_dimension=0, tiled=True),
        lax.psum_scatter(grad_shift_one, ("dp", "seq"), scatter_dimension=0, tiled=True),
        lax.psum_scatter(grad_bias_up, ("dp", "seq"), scatter_dimension=0, tiled=True),
        lax.psum_scatter(grad_bias_down, ("dp", "seq"), scatter_dimension=0, tiled=True),
        lax.psum_scatter(grad_gain_two, ("dp", "seq"), scatter_dimension=0, tiled=True),
        lax.psum_scatter(grad_shift_two, ("dp", "seq"), scatter_dimension=0, tiled=True),
    )
    return (
        layer_out,
        grad_input,
        sum_qkv,
        sum_bias_query,
        sum_bias_value,
        sum_out,
        sum_bias_out,
        sum_gain_one,
        sum_shift_one,
        sum_up,
        sum_bias_up,
        sum_down,
        sum_bias_down,
        sum_gain_two,
        sum_shift_two,
    )


def solution(mesh):
    in_specs = (
        P(("dp", "seq"), None),
        P(("dp", "seq"), None),
        P(("dp", "seq"), None),
        P(("dp", "seq")),
        P(("dp", "seq")),
        P(("dp", "seq"), None),
        P(("dp", "seq")),
        P(("dp", "seq")),
        P(("dp", "seq")),
        P(("dp", "seq"), None),
        P(("dp", "seq")),
        P(("dp", "seq"), None),
        P(("dp", "seq")),
        P(("dp", "seq")),
        P(("dp", "seq")),
    )
    out_specs = (
        P(("dp", "seq"), None),
        P(("dp", "seq"), None),
        P(("dp", "seq"), None),
        P(("dp", "seq")),
        P(("dp", "seq")),
        P(("dp", "seq"), None),
        P(("dp", "seq")),
        P(("dp", "seq")),
        P(("dp", "seq")),
        P(("dp", "seq"), None),
        P(("dp", "seq")),
        P(("dp", "seq"), None),
        P(("dp", "seq")),
        P(("dp", "seq")),
        P(("dp", "seq")),
    )
    return jax.shard_map(
        on_device, mesh=mesh, in_specs=in_specs, out_specs=out_specs, check_vma=False
    )
```

profile of v0, /device:TPU:0, one launch (start us, length us, event | category | flops | bytes accessed | tf_op | source)
XLA Modules:
  0.0 792.0 jit_solution(2282236051162359734)
XLA Ops:
  16.7 42.4 %all-reduce.18 = (bf16[1024]{0:T(1024)(128)(2,1)S(1)}, bf16[1024]{0:T(1024)(128)(2,1)S(1)}, bf16[1024]{0:T(1024)(128)(2,1)S(1)}, bf16[1024]{0:T(1024)(128)(2,1)S...) all-reduce(bf16[1024]{0:T(1024)(128)(2,1)S(1)} %dynamic-update-slic, ...), channel_id=1, replica_groups=mesh['dp'=8,'seq'=4] {'dp','seq'}, use_global_device_ids=true, to_apply=%add.1 | all-reduce | flops 8192 | bytes 32768
  59.1 23.9 %all-gather.10.cloned.1.call-done = bf16[1024,3072]{1,0:T(8,128)(2,1)} async-done(((bf16[32,3072]{1,0:T(8,128)(2,1)}), bf16[1024,3072]{1,0:T(8,128)(2,1)}) %all-gather.10.cloned.1.call-update) | async-done | bytes 6291472 | tf_op jit(solution)/shard_map/all_gather | solution.py:160
  93.3 15.7 %all-to-all-done = bf16[256,4,256]{0,2,1:T(8,128)(2,1)S(1)} async-done(((bf16[256,4,256]{0,2,1:T(8,128)(2,1)}), bf16[256,4,256]{0,2,1:T(8,128)(2,1)S(1)}, u32[]{:S(2)}, u32[]{:S(2)}) %all-to-all-start) | async-done | bytes 524320 | tf_op jit(solution)/shard_map/all_to_all | solution.py:186
  113.3 16.3 %all-to-all-done.1 = bf16[256,4,256]{2,0,1:T(8,128)(2,1)S(1)} async-done(((bf16[256,4,256]{2,0,1:T(8,128)(2,1)}), bf16[256,4,256]{2,0,1:T(8,128)(2,1)S(1)}, u32[]{:S(2)}, u32[]{:S(2)}) %all-to-all-start.1) | async-done | bytes 524320 | tf_op jit(solution)/shard_map/all_to_all | solution.py:187
  134.6 18.6 %all-to-all-done.2 = bf16[256,4,256]{2,0,1:T(8,128)(2,1)S(1)} async-done(((bf16[256,4,256]{2,0,1:T(8,128)(2,1)}), bf16[256,4,256]{2,0,1:T(8,128)(2,1)S(1)}, u32[]{:S(2)}, u32[]{:S(2)}) %all-to-all-start.2) | async-done | bytes 524320 | tf_op jit(solution)/shard_map/all_to_all | solution.py:194
  153.9 10.3 %while.27 = (s32[]{:T(128)}, bf16[2,512,4,64]{1,3,2,0:T(8,128)(2,1)S(1)}, f32[2,4,512]{2,1,0:T(4,128)S(1)}, bf16[2,512,4,64]{1,3,2,0:T(8,128)(2,1)S(1)}, bf16[10...) while((s32[]{:T(128)}, bf16[2,512,4,64]{1,3,2,0:T(8,128)(2,1)S(1)}, ...), condition=%wide.region_3.4_spmd, body=%wide.region_0.3_spmd.sunk | while | flops 553777152 | bytes 26804312 | solution.py:69
  167.7 19.6 %all_to_all.268 = bf16[4,256,256]{1,2,0:T(8,128)(2,1)} all-to-all(bf16[4,256,256]{1,2,0:T(8,128)(2,1)S(1)} %copy.119), channel_id=1, replica_groups=mesh['dp'=8,'seq'=4] {'seq'}, dimensions={0} | all-to-all | bytes 1048576 | tf_op jit(solution)/shard_map/all_to_all | solution.py:210
  188.0 65.6 %all-gather = bf16[32,1,128]{2,1,0:T(2,128)(2,1)S(1)} all-gather(bf16[1,1,128]{2,1,0:T(2,128)(2,1)S(1)} %bitcast.250), channel_id=1, replica_groups=mesh['dp'=8,'seq'=4] {'dp','seq'}, dimensions={0}, use_global_device_ids=true | all-gather | bytes 8448 | tf_op jit(solution)/shard_map/all_gather | solution.py:169
  256.9 8.5 %multiply_convert_fusion.1 = (bf16[256,4096]{1,0:T(8,128)(2,1)}, f32[256,4096]{1,0:T(8,128)}) fusion(f32[4096]{0:T(1024)S(1)} %bitcast.249, bf16[256,1024]{1,0:T(8,128)(2,1)S(1)} %fusion.54, bf16[1024,4096]{1,0:T(8,128)(2,1)} %all-gather.14.cloned.1.call-done), kind=kOutput, calls=%fused_computation.52 | convolution fusion | flops 2153775104 | bytes 15220736 | tf_op jit(solution)/shard_map/dot_general | solution.py:222
  265.4 47.6 %all-gather.16.cloned.1.call-done = bf16[1024,4096]{1,0:T(8,128)(2,1)} async-done(((bf16[32,4096]{1,0:T(8,128)(2,1)}), bf16[1024,4096]{1,0:T(8,128)(2,1)}) %all-gather.16.cloned.1.call-update) | async-done | bytes 8388624 | tf_op jit(solution)/shard_map/all_gather | solution.py:163
  312.9 6.6 fusion.61
  322.7 6.7 fusion.58
  329.4 6.9 multiply_reduce_fusion.1
  346.6 23.5 %all-to-all-done.4 = bf16[256,4,256]{0,2,1:T(8,128)(2,1)S(1)} async-done(((bf16[256,4,256]{0,2,1:T(8,128)(2,1)}), bf16[256,4,256]{0,2,1:T(8,128)(2,1)S(1)}, u32[]{:S(2)}, u32[]{:S(2)}) %all-to-all-start.4) | async-done | bytes 524320 | tf_op jit(solution)/shard_map/all_to_all | solution.py:256
  382.3 39.1 %while.28 = (s32[]{:T(128)}, f32[1024,4,64]{0,2,1:T(8,128)S(1)}, f32[1024,4,64]{0,2,1:T(8,128)}, bf16[2,512,4,64]{1,3,2,0:T(8,128)(2,1)}, bf16[2,512,4,64]{1,3,2...) while((s32[]{:T(128)}, f32[1024,4,64]{0,2,1:T(8,128)S(1)}, ...), condition=%wide.region_14.15_spmd.clone, body=%wide.region_13.14_spmd.clone.sunk | while | flops 1360527360 | bytes 111993552 | solution.py:116
  430.2 26.6 %all-to-all-done.5 = bf16[4,256,256]{1,2,0:T(8,128)(2,1)S(1)} async-done(((bf16[4,256,256]{1,2,0:T(8,128)(2,1)}), bf16[4,256,256]{1,2,0:T(8,128)(2,1)S(1)}, u32[]{:S(2)}, u32[]{:S(2)}) %all-to-all-start.5) | async-done | bytes 524320 | tf_op jit(solution)/shard_map/all_to_all | solution.py:261
  461.6 22.2 %all-to-all-done.7 = bf16[4,256,256]{1,2,0:T(8,128)(2,1)S(1)} async-done(((bf16[4,256,256]{1,2,0:T(8,128)(2,1)}), bf16[4,256,256]{1,2,0:T(8,128)(2,1)S(1)}, u32[]{:S(2)}, u32[]{:S(2)}) %all-to-all-start.7) | async-done | bytes 524320 | tf_op jit(solution)/shard_map/all_to_all | solution.py:267
  488.2 13.6 %all-to-all-done.6 = bf16[4,256,256]{1,2,0:T(8,128)(2,1)S(1)} async-done(((bf16[4,256,256]{1,2,0:T(8,128)(2,1)}), bf16[4,256,256]{1,2,0:T(8,128)(2,1)S(1)}, u32[]{:S(2)}, u32[]{:S(2)}) %all-to-all-start.6) | async-done | bytes 524320 | tf_op jit(solution)/shard_map/all_to_all | solution.py:264
  508.4 11.6 %all-to-all-done.10 = bf16[256,4,256]{2,0,1:T(8,128)(2,1)} async-done(((bf16[256,4,256]{2,0,1:T(8,128)(2,1)}), bf16[256,4,256]{2,0,1:T(8,128)(2,1)}, u32[]{:S(2)}, u32[]{:S(2)}) %all-to-all-start.10) | async-done | bytes 524320 | tf_op jit(solution)/shard_map/all_to_all | solution.py:283
  526.0 62.8 %all-to-all-done.8 = bf16[256,4,768]{2,0,1:T(8,128)(2,1)} async-done(((bf16[256,4,768]{2,0,1:T(8,128)(2,1)}), bf16[256,4,768]{2,0,1:T(8,128)(2,1)}, u32[]{:S(2)}, u32[]{:S(2)}) %all-to-all-start.8) | async-done | bytes 1572896 | tf_op jit(solution)/shard_map/all_to_all | solution.py:282
  606.2 35.8 %all-to-all-done.14 = bf16[256,4,1024]{2,0,1:T(8,128)(2,1)} async-done(((bf16[256,4,1024]{2,0,1:T(8,128)(2,1)}), bf16[256,4,1024]{2,0,1:T(8,128)(2,1)}, u32[]{:S(2)}, u32[]{:S(2)}) %all-to-all-start.14) | async-done | bytes 2097184 | tf_op jit(solution)/shard_map/all_to_all | solution.py:285
  651.9 41.5 %all-to-all-done.12 = bf16[256,4,1024]{2,0,1:T(8,128)(2,1)S(1)} async-done(((bf16[256,4,1024]{2,0,1:T(8,128)(2,1)}), bf16[256,4,1024]{2,0,1:T(8,128)(2,1)S(1)}, u32[]{:S(2)}, u32[]{:S(2)}) %all-to-all-start.12) | async-done | bytes 2097184 | tf_op jit(solution)/shard_map/all_to_all | solution.py:284
  724.4 41.5 %all-reduce.17 = (f32[1024]{0:T(1024)S(1)}, f32[1024]{0:T(1024)S(1)}, f32[1024]{0:T(1024)S(1)}, f32[1024]{0:T(1024)S(1)}, f32[1024]{0:T(1024)S(1)}, /*index=5*/f...) all-reduce(f32[1024]{0:T(1024)S(1)} %bitcast.247, ...), channel_id=3, replica_groups=mesh['dp'=8,'seq'=4] {'dp','seq'}, use_global_device_ids=true, to_apply=%region_17.18.clone | all-reduce | flops 12288 | bytes 98304
  777.1 7.0 all-to-all-done.13
  (235 shorter events, 212.1 us)
Async XLA Ops:
  7.2 75.9 %all-gather.10.cloned.1.call-start = ((), (), s32[]{:S(2)}) async-start(), calls=%async_computation.20 | async-start | bytes 6488064 | tf_op jit(solution)/shard_map/all_gather | solution.py:160
  7.9 245.8 %all-gather.12.cloned.1.call-start = ((), (), s32[]{:S(2)}) async-start(), calls=%async_computation.21 | async-start | bytes 2162688 | tf_op jit(solution)/shard_map/all_gather | solution.py:161
  8.7 248.2 %all-gather.14.cloned.1.call-start = ((), (), s32[]{:S(2)}) async-start(), calls=%async_computation.22 | async-start | bytes 8650752 | tf_op jit(solution)/shard_map/all_gather | solution.py:162
  9.4 303.5 %all-gather.16.cloned.1.call-start = ((), (), s32[]{:S(2)}) async-start(), calls=%async_computation.23 | async-start | bytes 8650752 | tf_op jit(solution)/shard_map/all_gather | solution.py:163
  89.0 20.0 %all-to-all-start = ((bf16[256,4,256]{0,2,1:T(8,128)(2,1)}), bf16[256,4,256]{0,2,1:T(8,128)(2,1)S(1)}, u32[]{:S(2)}, u32[]{:S(2)}) async-start(bf16[256,4,256]{0,2,1:T(8,128)(2,1)} %bitcast.4), calls=%async_computation | async-start | bytes 1048576 | tf_op jit(solution)/shard_map/all_to_all | solution.py:186
  109.0 20.6 %all-to-all-start.1 = ((bf16[256,4,256]{2,0,1:T(8,128)(2,1)}), bf16[256,4,256]{2,0,1:T(8,128)(2,1)S(1)}, u32[]{:S(2)}, u32[]{:S(2)}) async-start(bf16[256,4,256]{2,0,1:T(8,128)(2,1)} %bitcast.177), calls=%async_computation.1 | async-start | bytes 1048576 | tf_op jit(solution)/shard_map/all_to_all | solution.py:187
  129.6 23.6 %all-to-all-start.2 = ((bf16[256,4,256]{2,0,1:T(8,128)(2,1)}), bf16[256,4,256]{2,0,1:T(8,128)(2,1)S(1)}, u32[]{:S(2)}, u32[]{:S(2)}) async-start(bf16[256,4,256]{2,0,1:T(8,128)(2,1)} %bitcast.176), calls=%async_computation.2 | async-start | bytes 1048576 | tf_op jit(solution)/shard_map/all_to_all | solution.py:194
  133.0 460.5 %all-gather.20.cloned.1.call-start = ((), (), s32[]{:S(2)}) async-start(), calls=%async_computation.25 | async-start | bytes 2621440 | tf_op jit(solution)/shard_map/all_gather | solution.py:277
  187.4 409.5 %all-gather.18.cloned.1.call-start = ((), (), s32[]{:S(2)}) async-start(), calls=%async_computation.24 | async-start | bytes 2621440 | tf_op jit(solution)/shard_map/all_gather | solution.py:276
  340.3 29.8 %all-to-all-start.4 = ((bf16[256,4,256]{0,2,1:T(8,128)(2,1)}), bf16[256,4,256]{0,2,1:T(8,128)(2,1)S(1)}, u32[]{:S(2)}, u32[]{:S(2)}) async-start(bf16[256,4,256]{0,2,1:T(8,128)(2,1)} %bitcast.12), calls=%async_computation.4 | async-start | bytes 1048576 | tf_op jit(solution)/shard_map/all_to_all | solution.py:256
  343.8 301.9 %all-gather.24.cloned.1.call-start = ((), (), s32[]{:S(2)}) async-start(), calls=%async_computation.29 | async-start | bytes 2621440 | tf_op jit(solution)/shard_map/all_gather | solution.py:279
  424.1 32.7 %all-to-all-start.5 = ((bf16[4,256,256]{1,2,0:T(8,128)(2,1)}), bf16[4,256,256]{1,2,0:T(8,128)(2,1)S(1)}, u32[]{:S(2)}, u32[]{:S(2)}) async-start(bf16[4,256,256]{1,2,0:T(8,128)(2,1)} %copy.127), calls=%async_computation.5 | async-start | bytes 1048576 | tf_op jit(solution)/shard_map/all_to_all | solution.py:261
  456.8 27.0 %all-to-all-start.7 = ((bf16[4,256,256]{1,2,0:T(8,128)(2,1)}), bf16[4,256,256]{1,2,0:T(8,128)(2,1)S(1)}, u32[]{:S(2)}, u32[]{:S(2)}) async-start(bf16[4,256,256]{1,2,0:T(8,128)(2,1)} %copy.129), calls=%async_computation.7 | async-start | bytes 1048576 | tf_op jit(solution)/shard_map/all_to_all | solution.py:267
  483.8 18.0 %all-to-all-start.6 = ((bf16[4,256,256]{1,2,0:T(8,128)(2,1)}), bf16[4,256,256]{1,2,0:T(8,128)(2,1)S(1)}, u32[]{:S(2)}, u32[]{:S(2)}) async-start(bf16[4,256,256]{1,2,0:T(8,128)(2,1)} %copy.128), calls=%async_computation.6 | async-start | bytes 1048576 | tf_op jit(solution)/shard_map/all_to_all | solution.py:264
  501.8 18.2 %all-to-all-start.10 = ((bf16[256,4,256]{2,0,1:T(8,128)(2,1)}), bf16[256,4,256]{2,0,1:T(8,128)(2,1)}, u32[]{:S(2)}, u32[]{:S(2)}) async-start(bf16[256,4,256]{2,0,1:T(8,128)(2,1)} %bitcast.175), calls=%async_computation.10 | async-start | bytes 1048576 | tf_op jit(solution)/shard_map/all_to_all | solution.py:283
  506.0 146.0 %all-gather.22.cloned.1.call-start = ((), (), s32[]{:S(2)}) async-start(), calls=%async_computation.27 | async-start | bytes 2621440 | tf_op jit(solution)/shard_map/all_gather | solution.py:278
  520.1 68.7 %all-to-all-start.8 = ((bf16[256,4,768]{2,0,1:T(8,128)(2,1)}), bf16[256,4,768]{2,0,1:T(8,128)(2,1)}, u32[]{:S(2)}, u32[]{:S(2)}) async-start(bf16[256,4,768]{2,0,1:T(8,128)(2,1)} %copy.130), calls=%async_computation.8 | async-start | bytes 3145728 | tf_op jit(solution)/shard_map/all_to_all | solution.py:282
  588.8 53.2 %all-to-all-start.14 = ((bf16[256,4,1024]{2,0,1:T(8,128)(2,1)}), bf16[256,4,1024]{2,0,1:T(8,128)(2,1)}, u32[]{:S(2)}, u32[]{:S(2)}) async-start(bf16[256,4,1024]{2,0,1:T(8,128)(2,1)} %bitcast.173), calls=%async_computation.16 | async-start | bytes 4194304 | tf_op jit(solution)/shard_map/all_to_all | solution.py:285
  593.3 107.5 %reduce-scatter.7.cloned.1.call-start = ((), (), s32[]{:S(2)}) async-start(), calls=%async_computation.26 | async-start | bytes 589824 | tf_op jit(solution)/shard_map/reduce_scatter | solution.py:297
  596.8 113.1 %reduce-scatter.13.cloned.1.call-start = ((), (), s32[]{:S(2)}) async-start(), calls=%async_computation.31 | async-start | bytes 1769472 | tf_op jit(solution)/shard_map/reduce_scatter | solution.py:294
  642.0 51.4 %all-to-all-start.12 = ((bf16[256,4,1024]{2,0,1:T(8,128)(2,1)}), bf16[256,4,1024]{2,0,1:T(8,128)(2,1)S(1)}, u32[]{:S(2)}, u32[]{:S(2)}) async-start(bf16[256,4,1024]{2,0,1:T(8,128)(2,1)} %bitcast.174), calls=%async_computation.13 | async-start | bytes 4194304 | tf_op jit(solution)/shard_map/all_to_all | solution.py:284
  645.7 73.6 %reduce-scatter.11.cloned.1.call-start = ((), (), s32[]{:S(2)}) async-start(), calls=%async_computation.30 | async-start | bytes 2359296 | tf_op jit(solution)/shard_map/reduce_scatter | solution.py:303
  651.9 120.0 %reduce-scatter.9.cloned.1.call-start = ((), (), s32[]{:S(2)}) async-start(), calls=%async_computation.28 | async-start | bytes 2359296 | tf_op jit(solution)/shard_map/reduce_scatter | solution.py:300
  719.5 52.4 %all-to-all-start.15 = ((bf16[4,32,1024]{2,1,0:T(8,128)(2,1)}), bf16[4,32,1024]{2,1,0:T(8,128)(2,1)S(1)}, u32[]{:S(2)}, u32[]{:S(2)}) async-start(bf16[4,32,1024]{2,1,0:T(8,128)(2,1)} %bitcast.239), calls=%async_computation.18 | async-start | bytes 524288 | tf_op jit(solution)/shard_map/all_to_all | solution.py:317
  (26 other events, 417.4 us)
Sparse Core Ops, SparseCore 0:
  10.9 72.1 all-gather.9
  86.0 63.2 all-gather.11
  152.2 82.1 all-gather.13
  237.2 75.7 all-gather.15
  314.3 56.1 all-gather.19
  371.9 43.7 all-gather.17
  417.3 66.9 all-gather.23
  508.3 77.6 all-gather.21
  597.8 35.4 reduce-scatter.6
  636.4 38.3 reduce-scatter.12
  678.1 41.1 reduce-scatter.10
  722.4 41.1 reduce-scatter.8
where the time goes:
time: 805 us; the launch traced here: 792 us
  waiting for transfers between devices  377 us (47%)
  blocking collectives  169 us (21%)
  matrix products  102 us (13%)
  local copies, waits for them, and re-layouts  60 us (7%)
  starting transfers between devices  56.7 us (7%)
  between operations  15.2 us (2%)
  other arithmetic  11.8 us (1%)
    unnamed x2, blocking collectives  84 us
    all_gather x1, blocking collectives, on_device(): lax.all_gather(b_up, ('dp', 'seq'), axis=0, tiled=True)  65.6 us
    all_to_all x1, waiting for transfers between devices, on_device(): lax.all_to_all(grad_projected, 'seq', split_axis=1, concat_axis=0, tiled=...  62.8 us
    all_gather x1, waiting for transfers between devices, on_device(): lax.all_gather(w_down, ('dp', 'seq'), axis=0, tiled=True)  47.6 us
    all_to_all x1, waiting for transfers between devices, on_device(): lax.all_to_all(grad_inner_low, 'seq', split_axis=1, concat_axis=0, tiled=...  41.5 us
    all_to_all x1, waiting for transfers between devices, on_device(): lax.all_to_all(active_low, 'seq', split_axis=1, concat_axis=0, tiled=True)  35.8 us
    all_to_all x1, waiting for transfers between devices, on_device(): lax.all_to_all(grad_query.reshape(length, group_cols), 'seq', split_axis=...  26.6 us
    all_gather x1, waiting for transfers between devices, on_device(): lax.all_gather(w_qkv, ('dp', 'seq'), axis=0, tiled=True)  23.9 us
  transfers between devices with their start and end apart: 27, of which 17 were waited for; matrix products, arithmetic and copies ran while one was open for 20% of the time, Pallas kernels for 0%

commit v1 on v0

v1 whole, which is shorter than its diff:
```python
import functools
import math

import jax
import jax.numpy as jnp
from jax import lax
from jax.experimental import pallas as pl
from jax.experimental.pallas import tpu as pltpu
from jax.sharding import Mesh
from jax.sharding import PartitionSpec as P

HD = 64
EPS = 1e-12
ALL = ("y", "x", "core", "seq")
BF16 = jnp.bfloat16
F32 = jnp.float32


def layer_norm(residual, gain_vec, shift_vec):
    row_mean = jnp.mean(residual, -1, keepdims=True)
    centred = residual - row_mean
    variance = jnp.mean(centred * centred, -1, keepdims=True)
    inv_std = lax.rsqrt(variance + EPS)
    normed = centred * inv_std
    return (normed * gain_vec + shift_vec, normed, inv_std)


def norm_back(incoming, normed, inv_std, gain_vec):
    scaled = incoming * gain_vec
    return inv_std * (
        scaled
        - jnp.mean(scaled, -1, keepdims=True)
        - normed * jnp.mean(scaled * normed, -1, keepdims=True)
    )


def gelu_both(inner):
    normal_cdf = 0.5 * (1.0 + jax.scipy.special.erf(inner / math.sqrt(2.0)))
    gelu_value = inner * normal_cdf
    gelu_slope = normal_cdf + inner * jnp.exp(-0.5 * inner * inner) / math.sqrt(2.0 * math.pi)
    return (gelu_value, gelu_slope)


def dot(left, right):
    return jnp.dot(left, right, preferred_element_type=F32)


def contract_last(left, right):
    return lax.dot_general(left, right, (((1,), (1,)), ((), ())), preferred_element_type=F32)


def contract_first(left, right):
    return lax.dot_general(left, right, (((0,), (0,)), ((), ())), preferred_element_type=F32)


def lanes_of(head, shape):
    lane = lax.broadcasted_iota(jnp.int32, shape, len(shape) - 1)
    return (lane >= head * HD) & (lane < (head + 1) * HD)


def forward_kernel(score_scale, query_ref, key_ref, value_ref, out_ref, total_ref, value_t, out_t):
    head = pl.program_id(1)

    @pl.when((pl.program_id(0) == 0) & (head == 0))
    def _():
        value_t[...] = value_ref[...].astype(F32).T.astype(BF16)

    query = query_ref[...]
    query = jnp.where(lanes_of(head, query.shape), query, jnp.zeros_like(query))
    scores = contract_last(key_ref[...], query) * score_scale
    top = jnp.max(scores, 0, keepdims=True)
    weights = jnp.exp(scores - top)
    total = jnp.sum(weights, 0, keepdims=True)
    total_ref[pl.ds(head, 1), :] = top + jnp.log(total)
    probs = (weights * (1.0 / total)).astype(BF16)
    rows = pl.ds(pl.multiple_of(head * HD, HD), HD)
    out_t[rows, :] = dot(value_t[rows, :], probs)

    @pl.when(head == pl.num_programs(1) - 1)
    def _():
        out_ref[...] = out_t[...].T.astype(BF16)


def attend_forward(projected):
    length, width = projected.shape[0], projected.shape[1] // 3
    block = min(256, length)
    heads = width // HD
    return pl.pallas_call(
        functools.partial(forward_kernel, 1.0 / math.sqrt(HD)),
        grid=(length // block, heads),
        in_specs=[
            pl.BlockSpec((block, width), lambda i, h: (i, 0)),
            pl.BlockSpec((length, width), lambda i, h: (0, 1)),
            pl.BlockSpec((length, width), lambda i, h: (0, 2)),
        ],
        out_specs=[
            pl.BlockSpec((block, width), lambda i, h: (i, 0)),
            pl.BlockSpec((heads, block), lambda i, h: (0, i)),
        ],
        out_shape=[
            jax.ShapeDtypeStruct((length, width), BF16),
            jax.ShapeDtypeStruct((heads, length), F32),
        ],
        scratch_shapes=[pltpu.VMEM((width, length), BF16), pltpu.VMEM((width, block), F32)],
        compiler_params=pltpu.CompilerParams(vmem_limit_bytes=24 * 2**20),
        cost_estimate=pl.CostEstimate(
            flops=4 * length * length * width,
            bytes_accessed=8 * length * width,
            transcendentals=heads * length * length,
        ),
        name="attend_forward",
    )(projected, projected, projected)


def backward_kernel(score_scale, block, query_ref, key_ref, value_ref, out_ref, total_ref,
                    grad_ref, result_ref, key_t, delta, query_t):
    step, head = pl.program_id(0), pl.program_id(1)
    width = query_ref.shape[1]
    heads = width // HD
    blocks = key_t.shape[0]

    @pl.when((step == 0) & (head == 0))
    def _():
        for number in range(blocks):
            key_t[number] = key_ref[pl.ds(number * block, block), :].astype(F32).T.astype(BF16)
        product = (grad_ref[...].astype(F32) * out_ref[...].astype(F32)).T
        for number in range(heads):
            delta[pl.ds(number, 1), :] = jnp.sum(
                product[number * HD : (number + 1) * HD], 0, keepdims=True
            )

    here = pl.ds(pl.multiple_of(step * block, block), block)
    mask = lanes_of(head, (block, width))
    key, value = key_ref[here, :], value_ref[here, :]
    key = jnp.where(mask, key, jnp.zeros_like(key))
    value = jnp.where(mask, value, jnp.zeros_like(value))
    scores = contract_last(key, query_ref[...]) * score_scale
    probs = jnp.exp(scores - total_ref[pl.ds(head, 1), :])
    grad_value = dot(probs.astype(BF16), grad_ref[...])
    grad_probs = contract_last(value, grad_ref[...])
    grad_scores = (probs * (grad_probs - delta[pl.ds(head, 1), :])).astype(BF16)
    grad_key = dot(grad_scores, query_ref[...]) * score_scale
    rows = pl.ds(pl.multiple_of(head * HD, HD), HD)
    part = dot(key_t[step, rows, :], grad_scores)

    @pl.when(step == 0)
    def _():
        query_t[rows, :] = part

    @pl.when(step > 0)
    def _():
        query_t[rows, :] += part

    for place, piece in ((width, grad_key), (2 * width, grad_value)):
        low = piece.astype(BF16)
        held = result_ref[here, place : place + width]
        result_ref[here, place : place + width] = jnp.where(mask, low, held)

    @pl.when((step == pl.num_programs(0) - 1) & (head == heads - 1))
    def _():
        result_ref[:, :width] = (query_t[...] * score_scale).T.astype(BF16)


def attend_backward(projected, outputs, log_total, grad_out):
    length, width = outputs.shape
    block = min(256, length)
    heads = width // HD
    full = pl.BlockSpec((length, width), lambda i, h: (0, 0))
    return pl.pallas_call(
        functools.partial(backward_kernel, 1.0 / math.sqrt(HD), block),
        grid=(length // block, heads),
        in_specs=[
            full,
            pl.BlockSpec((length, width), lambda i, h: (0, 1)),
            pl.BlockSpec((length, width), lambda i, h: (0, 2)),
            full,
            pl.BlockSpec((heads, length), lambda i, h: (0, 0)),
            full,
        ],
        out_specs=pl.BlockSpec((length, 3 * width), lambda i, h: (0, 0)),
        out_shape=jax.ShapeDtypeStruct((length, 3 * width), BF16),
        scratch_shapes=[
            pltpu.VMEM((length // block, width, block), BF16),
            pltpu.VMEM((heads, length), F32),
            pltpu.VMEM((width, length), F32),
        ],
        compiler_params=pltpu.CompilerParams(vmem_limit_bytes=32 * 2**20),
        cost_estimate=pl.CostEstimate(
            flops=10 * length * length * width,
            bytes_accessed=16 * length * width,
            transcendentals=heads * length * length,
        ),
        name="attend_backward",
    )(projected, projected, projected, outputs, log_total, grad_out)


def shift(block, axis, size, distance):
    return lax.ppermute(block, axis, [(i, (i + distance) % size) for i in range(size)])


def after(value, *earlier):
    return lax.optimization_barrier((value,) + earlier)[0]


def shifts(block, axis, size):
    return [shift(block, axis, size, size - d) for d in range(1, size)]


def in_order(block, others, axis, size, dim):
    if size == 1:
        return jnp.expand_dims(block, dim)
    me = lax.axis_index(axis)
    if size == 2:
        low = jnp.where(me == 0, block, others[0])
        high = jnp.where(me == 0, others[0], block)
        return jnp.stack([low, high], dim)
    ahead = [block] + list(others)
    twice = jnp.stack(ahead + ahead, dim)
    return lax.dynamic_slice_in_dim(twice, lax.rem(size - me, size), size, dim)


def gather_blocks(block, axis, size, dim):
    return in_order(block, shifts(block, axis, size), axis, size, dim)


def pick(blocks, index, dim):
    if blocks.shape[dim] == 2:
        first = lax.index_in_dim(blocks, 0, dim, keepdims=False)
        second = lax.index_in_dim(blocks, 1, dim, keepdims=False)
        return jnp.where(index == 0, first, second)
    return lax.dynamic_index_in_dim(blocks, index, dim, keepdims=False)


def reduce_blocks(blocks, axis, size, dim):
    me = lax.axis_index(axis)
    total = pick(blocks, me, dim).astype(F32)
    for distance in range(1, size):
        sent = pick(blocks, lax.rem(me + distance, size), dim).astype(BF16)
        total = total + shift(sent, axis, size, distance).astype(F32)
    return total


def body(sizes, hidden_states, cotangent, w_qkv, b_query, b_value, w_out, b_out, ln1_gain,
         ln1_shift, w_up, b_up, w_down, b_down, ln2_gain, ln2_shift):
    ny, nx, nc, ns = sizes
    devices = ny * nx * nc * ns
    rows, width = w_out.shape
    tokens = hidden_states.shape[0]
    inner_width = w_up.shape[1]
    own = width // ns
    seq_at = lax.axis_index("seq")
    core_at = lax.axis_index("core")

    def halves(matrix):
        half = matrix.shape[-1] // nc
        parts = matrix.reshape(matrix.shape[:-1] + (nc, half))
        return pick(parts, core_at, parts.ndim - 2), pick(parts, nc - 1 - core_at, parts.ndim - 2)

    def swap(block):
        return shift(block, "core", nc, 1)

    def pair(block):
        return jnp.concatenate([block, swap(block)], 0)

    def own_tokens(part):
        return part[:tokens] + swap(part[tokens:])

    def own_columns(shard):
        kept, sent = halves(shard)
        return in_order(kept, [swap(sent)], "core", nc, 0)

    def line_of(block, others):
        line = in_order(block, others, "seq", ns, 1)
        return line.reshape(block.shape[0], ns * block.shape[1], block.shape[2])

    def plane_of(line):
        low_x = shifts(line[0], "x", nx)
        high_y = shifts(line[1], "y", ny)
        low = in_order(line[0], low_x, "x", nx, 0)
        high = in_order(line[1], high_y, "y", ny, 0)
        low_y = shifts(low, "y", ny)
        high_x = shifts(high, "x", nx)
        low = in_order(low, low_y, "y", ny, 0)
        high = in_order(high, high_x, "x", nx, 1)
        return jnp.stack([low, high], 2).reshape(ny * nx * nc * line.shape[1], line.shape[2])

    def over_plane(full):
        line_rows = full.shape[0] // (ny * nx * nc)
        parts = full.reshape(ny, nx, nc, line_rows, full.shape[1])
        low = reduce_blocks(parts[:, :, 0], "x", nx, 1).astype(BF16)
        high = reduce_blocks(parts[:, :, 1], "y", ny, 0).astype(BF16)
        low = reduce_blocks(low, "y", ny, 0).astype(BF16)
        high = reduce_blocks(high, "x", nx, 0).astype(BF16)
        return jnp.stack([low, high], 0)

    def over_line(part):
        blocks = part.reshape(nc, ns, part.shape[1] // ns, part.shape[2])
        total = reduce_blocks(blocks, "seq", ns, 1)
        kept = pick(total, core_at, 0)
        came = swap(pick(total, nc - 1 - core_at, 0).astype(BF16)).astype(F32)
        low = jnp.where(core_at == 0, kept, came)
        high = jnp.where(core_at == 0, came, kept)
        return jnp.concatenate([low, high], 1)

    small = (b_query, b_value, b_out, ln1_gain, ln1_shift, b_up, b_down, ln2_gain, ln2_shift)
    packed = jnp.concatenate(small)[None]
    packed = lax.all_to_all(
        jnp.tile(packed, (devices, 1)), ALL, split_axis=0, concat_axis=0, tiled=True
    ).astype(F32)
    vectors, place = [], 0
    for shard in small:
        vectors.append(packed[:, place : place + shard.shape[0]].reshape(-1))
        place += shard.shape[0]
    (bias_query, bias_value, bias_out, gain_one, shift_one, bias_up, bias_down, gain_two,
     shift_two) = vectors

    by_owner = w_qkv.reshape(rows, 3, ns, own).transpose(0, 2, 1, 3).reshape(rows, 3 * width)
    to_owner = by_owner.reshape(rows, ns, 3 * own)
    kept = lax.dynamic_index_in_dim(to_owner, seq_at, 1, keepdims=False)
    came = [
        shift(
            lax.dynamic_index_in_dim(to_owner, lax.rem(seq_at + ns - d, ns), 1, keepdims=False),
            "seq", ns, ns - d,
        )
        for d in range(1, ns)
    ]
    own_line = in_order(kept, came, "seq", ns, 0).reshape(ns * rows, 3 * own)
    plane = gather_blocks(gather_blocks(own_line, "x", nx, 0), "y", ny, 0)
    own_qkv = gather_blocks(plane, "core", nc, 2).reshape(width, 3 * own)

    up_out = own_columns(w_up), own_columns(w_out)
    up_out = after(jnp.concatenate(up_out, 2), *came)
    up_line = shifts(up_out, "seq", ns)
    hidden_sent = after(hidden_states, *up_line)
    hidden_line = shifts(hidden_sent, "seq", ns)
    seq_hidden = in_order(hidden_sent, hidden_line, "seq", ns, 0).reshape(ns * tokens, width)
    down_own = after(own_columns(w_down), *hidden_line)
    down_line = shifts(down_own, "seq", ns)
    half_up_out = plane_of(after(line_of(up_out, up_line), own_qkv))
    half = inner_width // nc
    half_up, half_out = half_up_out[:, :half], half_up_out[:, half:]
    other_out = swap(half_out)
    half_down = plane_of(after(line_of(down_own, down_line), half_up_out))

    own_bias = jnp.concatenate(
        [
            lax.dynamic_slice_in_dim(bias_query, seq_at * own, own),
            jnp.zeros((own,), F32),
            lax.dynamic_slice_in_dim(bias_value, seq_at * own, own),
        ]
    )
    projected = (dot(seq_hidden, own_qkv) + own_bias).astype(BF16)
    outputs, log_total = attend_forward(projected)
    attn_tok = lax.all_to_all(outputs, "seq", split_axis=0, concat_axis=1, tiled=True)
    qkv_own = after(own_columns(by_owner), attn_tok)
    qkv_line = shifts(qkv_own, "seq", ns)
    half_qkv = plane_of(after(line_of(qkv_own, qkv_line), half_down))
    other_qkv = swap(half_qkv)

    mixed, mixed_other = dot(attn_tok, half_out), dot(attn_tok, other_out)
    mixed = jnp.concatenate(
        [
            jnp.where(core_at == 0, mixed, mixed_other),
            jnp.where(core_at == 0, mixed_other, mixed),
        ],
        1,
    )
    resid_one = hidden_states.astype(F32) + mixed + bias_out
    hidden_one, normed_one, inv_one = layer_norm(resid_one, gain_one, shift_one)
    hidden_low = hidden_one.astype(BF16)

    hidden_two = pair(hidden_low)
    gelu_value, gelu_slope = gelu_both(dot(hidden_two, half_up) + halves(bias_up)[0])
    active_low = gelu_value.astype(BF16)
    resid_two = hidden_one + own_tokens(contract_last(active_low, half_down))
    layer_val, normed_two, inv_two = layer_norm(resid_two + bias_down, gain_two, shift_two)
    layer_out = layer_val.astype(BF16)

    grad_y = cotangent.astype(F32)
    grad_gain_two = jnp.sum(grad_y * normed_two, 0)
    grad_shift_two = jnp.sum(grad_y, 0)
    grad_resid_two = norm_back(grad_y, normed_two, inv_two, gain_two)
    grad_low_two = pair(grad_resid_two.astype(BF16))
    grad_bias_down = jnp.sum(grad_resid_two, 0)
    sum_down = contract_first(grad_low_two, active_low).astype(BF16)
    sum_down = over_plane(sum_down)
    grad_inner = dot(grad_low_two, half_down) * gelu_slope
    grad_inner_low = grad_inner.astype(BF16)
    grad_bias_up = jnp.sum(grad_inner, 0)
    grad_hidden = grad_resid_two + own_tokens(contract_last(grad_inner_low, half_up))
    sum_up = contract_first(hidden_two, grad_inner_low).astype(BF16)
    sum_up = over_plane(after(sum_up, sum_down))
    grad_gain_one = jnp.sum(grad_hidden * normed_one, 0)
    grad_shift_one = jnp.sum(grad_hidden, 0)
    grad_resid_one = norm_back(grad_hidden, normed_one, inv_one, gain_one)
    grad_low_one = grad_resid_one.astype(BF16)
    grad_bias_out = jnp.sum(grad_resid_one, 0)
    grad_kept, grad_sent = halves(grad_low_one)
    grad_attn = (
        contract_last(grad_kept, half_out) + contract_last(grad_sent, other_out)
    ).astype(BF16)
    grad_attn_cols = lax.all_to_all(grad_attn, "seq", split_axis=1, concat_axis=0, tiled=True)
    grad_out_two = jnp.concatenate([grad_kept, swap(grad_sent)], 0)
    sum_out = contract_first(pair(attn_tok), grad_out_two).astype(BF16)
    sum_out = over_plane(after(sum_out, sum_up))

    grad_own = attend_backward(projected, outputs, log_total, grad_attn_cols)
    grad_tok = lax.all_to_all(grad_own, "seq", split_axis=0, concat_axis=1, tiled=True)
    own_kept, own_sent = halves(grad_own)
    other_sum = swap(contract_first(seq_hidden, own_sent).astype(BF16))
    sum_qkv = (contract_first(seq_hidden, own_kept) + other_sum.astype(F32)).astype(BF16)
    sum_qkv = over_plane(sum_qkv)
    to_core = pick(sum_qkv, nc - 1 - core_at, 0)
    sum_qkv = in_order(
        pick(sum_qkv, core_at, 0), [swap(to_core)], "core", nc, 1
    ).reshape(ns, rows, 3 * own)
    sum_qkv = in_order(
        pick(sum_qkv, seq_at, 0),
        [
            shift(pick(sum_qkv, lax.rem(seq_at + ns - d, ns), 0), "seq", ns, ns - d)
            for d in range(1, ns)
        ],
        "seq", ns, 0,
    )
    sum_qkv = sum_qkv.astype(F32).reshape(ns, rows, 3, own).transpose(1, 2, 0, 3)
    sum_qkv = sum_qkv.reshape(rows, 3 * width)
    tok_kept, tok_other = halves(grad_tok)
    grad_input = (
        grad_resid_one + contract_last(tok_kept, half_qkv) + contract_last(tok_other, other_qkv)
    )
    sum_down = over_line(after(sum_down, grad_attn_cols))
    sum_up = over_line(sum_up)
    sum_out = over_line(sum_out)

    def spread(part, whole, start):
        return lax.dynamic_update_slice_in_dim(jnp.zeros((whole,), F32), part, start, 0)

    own_sums = jnp.sum(grad_own.astype(F32), 0)

    def sum_small(parts):
        stacked = jnp.concatenate([part.reshape(devices, -1) for part in parts], 1)
        arrived = lax.all_to_all(stacked, ALL, split_axis=0, concat_axis=0, tiled=True)
        total = jnp.sum(arrived, 0)
        ends, place = [], 0
        for part in parts:
            count = part.shape[0] // devices
            ends.append(total[place : place + count])
            place += count
        return ends

    (sum_gain_two, sum_shift_two, sum_bias_down, sum_bias_up, sum_gain_one, sum_shift_one,
     sum_bias_out) = sum_small(
        (grad_gain_two, grad_shift_two, grad_bias_down,
         spread(grad_bias_up, inner_width, core_at * half), grad_gain_one, grad_shift_one,
         grad_bias_out)
    )
    sum_bias_query, sum_bias_value = sum_small(
        (spread(own_sums[:own], width, seq_at * own),
         spread(own_sums[2 * own :], width, seq_at * own))
    )
    return (layer_out, grad_input, sum_qkv, sum_bias_query, sum_bias_value, sum_out, sum_bias_out,
            sum_gain_one, sum_shift_one, sum_up, sum_bias_up, sum_down, sum_bias_down,
            sum_gain_two, sum_shift_two)


def solution(mesh):
    dp, ns = mesh.shape["dp"], mesh.shape["seq"]
    nc = 2
    ny = 2 if (dp // nc) % 2 == 0 else 1
    sizes = (ny, dp // (nc * ny), nc, ns)
    fine = Mesh(mesh.devices.reshape(sizes), ALL)
    matrix, vector = P(ALL, None), P(ALL)
    in_specs = (matrix, matrix, matrix, vector, vector, matrix, vector, vector, vector, matrix,
                vector, matrix, vector, vector, vector)
    out_specs = (matrix, matrix, matrix, vector, vector, matrix, vector, vector, vector, matrix,
                 vector, matrix, vector, vector, vector)

    def on_device(*args):
        return body(sizes, *args)

    return jax.shard_map(
        on_device, mesh=fine, in_specs=in_specs, out_specs=out_specs, check_vma=False
    )
```

time: 805 us -> 513 us (0.64)
  blocking collectives: 169 us -> 0 us
  waiting for transfers between devices: 377 us -> 230 us
  matrix products: 102 us -> 45 us
  starting transfers between devices: 56.7 us -> 96.9 us
  other arithmetic: 11.8 us -> 48.1 us
  Pallas kernels: 0 us -> 32.1 us
  between operations: 15.2 us -> 3.17 us
  local copies, waits for them, and re-layouts: 60 us -> 48.1 us
    all_to_all x15 -> x6, waiting for transfers between devices: 301 us -> 9.71 us  [the longest x1 9.69 us: body(): lax.all_to_all(outputs, 'seq', split_axis=0, concat_axis=1, tiled=True)]
    ppermute x0 -> x75, waiting for transfers between devices: none -> 220 us  [shift(): lax.ppermute(block, axis, [(i, (i + distance) % size) for i in range(size)])]
    unnamed x2 -> x0, blocking collectives: 84 us -> none
    all_gather x8 -> x0, waiting for transfers between devices: 71.6 us -> none  [the longest x1 47.6 us: on_device(): lax.all_gather(w_down, ('dp', 'seq'), axis=0, tiled=True)]
    ppermute x0 -> x75, starting transfers between devices: none -> 66.9 us  [shift(): lax.ppermute(block, axis, [(i, (i + distance) % size) for i in range(size)])]
    all_gather x1 -> x0, blocking collectives: 65.6 us -> none  [on_device(): lax.all_gather(b_up, ('dp', 'seq'), axis=0, tiled=True)]
    dot_general x18 -> x5, matrix products: 61.7 us -> 14.2 us  [dot(): return jnp.dot(left, right, preferred_element_type=F32)]
    pallas_call x0 -> x2, Pallas kernels: none -> 32.1 us  [the longest x1 16.2 us: attend_backward(): pl.pallas_call(functools.partial(backward_kernel, 1.0 / math.sqrt(HD), bl...]
  transfers between devices with their start and end apart: 27 -> 81, of which waited for: 17 -> 37; matrix products, arithmetic and copies ran while one was open for 20% -> 22% of each run, Pallas kernels for 0% -> 6%
where the time goes in v1:
time: 513 us; the launch traced here: 503 us
  waiting for transfers between devices  230 us (45%)
  starting transfers between devices  96.9 us (19%)
  local copies, waits for them, and re-layouts  48.1 us (9%)
  other arithmetic  48.1 us (9%)
  matrix products  45 us (9%)
  Pallas kernels  32.1 us (6%)
    ppermute x75, waiting for transfers between devices, shift(): lax.ppermute(block, axis, [(i, (i + distance) % size) for i in range(size)])  220 us
    ppermute x75, starting transfers between devices, shift(): lax.ppermute(block, axis, [(i, (i + distance) % size) for i in range(size)])  66.9 us
    pallas_call x1, Pallas kernels, attend_backward(): pl.pallas_call(functools.partial(backward_kernel, 1.0 / math.sqrt(HD), bl...  16.2 us
    dot_general x5, matrix products, contract_first(): lax.dot_general(left, right, (((0,), (0,)), ((), ())), preferred_element_...  16 us
    pallas_call x1, Pallas kernels, attend_forward(): pl.pallas_call(functools.partial(forward_kernel, 1.0 / math.sqrt(HD)), gr...  15.9 us
    dot_general x6, matrix products, contract_last(): lax.dot_general(left, right, (((1,), (1,)), ((), ())), preferred_element_...  14.8 us
    dot_general x5, matrix products, dot(): return jnp.dot(left, right, preferred_element_type=F32)  14.2 us
    another operation x30, other arithmetic, in_order(): return jnp.stack([low, high], dim)  14 us
  transfers between devices with their start and end apart: 81, of which 37 were waited for; matrix products, arithmetic and copies ran while one was open for 22% of the time, Pallas kernels for 6%

profile of v1, /device:TPU:0, one launch (start us, length us, event | category | flops | bytes accessed | tf_op | source)
XLA Modules:
  0.0 503.0 jit_solution(17312130706188629993)
XLA Ops:
  0.6 6.1 %concatenate.42 = bf16[384]{0:T(512)(128)(2,1)S(1)} concatenate(bf16[32]{0:T(256)(128)(2,1)} %param.18, bf16[32]{0:T(256)(128)(2,1)} %param.19, bf16[32]{0:T(256)(128)(2,1)} %param.21, bf16[32]{0:T(256)(128)(2,1)} %param.22, bf16[32]{0:T(256)(128)(2,1)} %param.23, bf16[128]{0:T(256)(128)(2,1)} %param.25, bf16[32]{0:T(256)(128)(2,1)} %param.27, bf16[32]{0:T(256)(128)(2,1)} %param.28, ...), dimensions={0} | concatenate | bytes 1536 | tf_op jit(solution)/shard_map/concatenate | solution.py:306
  8.8 7.3 %all-to-all-start = ((bf16[32,2,192]{2,1,0:T(2,128)(2,1)}), bf16[32,2,192]{2,1,0:T(2,128)(2,1)S(1)}, u32[]{:S(2)}, u32[]{:S(2)}) async-start(bf16[32,2,192]{2,1,0:T(2,128)(2,1)} %reshape.456), calls=%async_computation | async-start | bytes 65536 | tf_op jit(solution)/shard_map/all_to_all | solution.py:307
  39.0 4.3 collective-permute-done.5
  43.3 20.6 %collective-permute-done.6 = bf16[2,32,2560]{2,1,0:T(8,128)(2,1)S(1)} collective-permute-done((bf16[2,32,2560]{2,1,0:T(8,128)(2,1)S(1)}, bf16[2,32,2560]{2,1,0:T(8,128)(2,1)S(1)}, u32[]{:S(2)}, u32[]{:S(2)}) %collective-permute-start.6) | collective-permute-done | bytes 327712 | tf_op jit(solution)/shard_map/ppermute | solution.py:198
  68.6 8.1 %collective-permute-done.8 = bf16[256,1024]{1,0:T(8,128)(2,1)S(1)} collective-permute-done((bf16[256,1024]{1,0:T(8,128)(2,1)S(1)}, bf16[256,1024]{1,0:T(8,128)(2,1)S(1)}, u32[]{:S(2)}, u32[]{:S(2)}) %collective-permute-start.8) | collective-permute-done | bytes 524320 | tf_op jit(solution)/shard_map/ppermute | solution.py:198
  76.7 35.0 %collective-permute-done.9 = bf16[256,1024]{1,0:T(8,128)(2,1)S(1)} collective-permute-done((bf16[256,1024]{1,0:T(8,128)(2,1)S(1)}, bf16[256,1024]{1,0:T(8,128)(2,1)S(1)}, u32[]{:S(2)}, u32[]{:S(2)}) %collective-permute-start.9) | collective-permute-done | bytes 524320 | tf_op jit(solution)/shard_map/ppermute | solution.py:198
  114.3 6.4 %collective-permute-done.21 = bf16[2,32,2048]{2,1,0:T(8,128)(2,1)S(1)} collective-permute-done((bf16[2,32,2048]{2,1,0:T(8,128)(2,1)S(1)}, bf16[2,32,2048]{2,1,0:T(8,128)(2,1)S(1)}, u32[]{:S(2)}, u32[]{:S(2)}) %collective-permute-start.21) | collective-permute-done | bytes 262176 | tf_op jit(solution)/shard_map/ppermute | solution.py:198
  120.7 14.3 %collective-permute-done.22 = bf16[2,32,2048]{2,1,0:T(8,128)(2,1)S(1)} collective-permute-done((bf16[2,32,2048]{2,1,0:T(8,128)(2,1)S(1)}, bf16[2,32,2048]{2,1,0:T(8,128)(2,1)S(1)}, u32[]{:S(2)}, u32[]{:S(2)}) %collective-permute-start.22) | collective-permute-done | bytes 262176 | tf_op jit(solution)/shard_map/ppermute | solution.py:198
  142.8 15.9 %attend_forward.1 = (bf16[1024,256]{1,0:T(8,128)(2,1)S(1)}, f32[4,1024]{1,0:T(4,128)S(1)}) custom-call(bf16[1024,768]{1,0:T(8,128)(2,1)S(1)} %add_convert_fusion.query_ref.key_ref.value_ref, bf16[1024,768]{1,0:T(8,128)(2,1)S(1)} %add_convert_fusion.query_ref.key_ref.value_ref, bf16[1024,768]{1,0:T(8,128)(2,1)S(1)} %add_convert_fusion.query_ref.key_ref.value_ref), custom_call_target="tpu_custom_call" | custom-call | flops 1073741824 | bytes 2097152 | tf_op jit(solution)/shard_map/attend_forward/pallas_call | solution.py:88
  168.5 9.7 %all-to-all-done.1 = bf16[4,256,256]{1,2,0:T(8,128)(2,1)} async-done(((bf16[4,256,256]{1,2,0:T(8,128)(2,1)}), bf16[4,256,256]{1,2,0:T(8,128)(2,1)}, u32[]{:S(2)}, u32[]{:S(2)}) %all-to-all-start.1) | async-done | bytes 524320 | tf_op jit(solution)/shard_map/all_to_all | solution.py:354
  184.8 9.6 %collective-permute-done.33 = bf16[2,32,1536]{2,1,0:T(8,128)(2,1)S(1)} collective-permute-done((bf16[2,32,1536]{2,1,0:T(8,128)(2,1)S(1)}, bf16[2,32,1536]{2,1,0:T(8,128)(2,1)S(1)}, u32[]{:S(2)}, u32[]{:S(2)}) %collective-permute-start.33) | collective-permute-done | bytes 196640 | tf_op jit(solution)/shard_map/ppermute | solution.py:198
  205.5 9.1 %collective-permute-done.24 = bf16[128,2048]{1,0:T(8,128)(2,1)S(1)} collective-permute-done((bf16[128,2048]{1,0:T(8,128)(2,1)S(1)}, bf16[128,2048]{1,0:T(8,128)(2,1)S(1)}, u32[]{:S(2)}, u32[]{:S(2)}) %collective-permute-start.24) | collective-permute-done | bytes 524320 | tf_op jit(solution)/shard_map/ppermute | solution.py:198
  220.1 17.1 %collective-permute-done.27 = bf16[2,128,2048]{2,1,0:T(8,128)(2,1)S(1)} collective-permute-done((bf16[2,128,2048]{2,1,0:T(8,128)(2,1)S(1)}, bf16[2,128,2048]{2,1,0:T(8,128)(2,1)S(1)}, u32[]{:S(2)}, u32[]{:S(2)}) %collective-permute-start.27) | collective-permute-done | bytes 1048608 | tf_op jit(solution)/shard_map/ppermute | solution.py:198
  263.4 9.9 %collective-permute-done.38 = bf16[2,128,1536]{2,1,0:T(8,128)(2,1)} collective-permute-done((bf16[2,128,1536]{2,1,0:T(8,128)(2,1)}, bf16[2,128,1536]{2,1,0:T(8,128)(2,1)}, u32[]{:S(2)}, u32[]{:S(2)}) %collective-permute-start.38) | collective-permute-done | bytes 786464 | tf_op jit(solution)/shard_map/ppermute | solution.py:198
  281.5 5.1 %fusion.129 = (f32[2048]{0:T(1024)S(1)}, bf16[512,2048]{1,0:T(8,128)(2,1)S(1)}) fusion(f32[512,2048]{1,0:T(8,128)S(1)} %copy-done.48, f32[2048]{0:T(1024)S(1)} %copy-done.43, bf16[1024,2048]{1,0:T(8,128)(2,1)S(1)} %bitcast.570, bf16[256,1024]{1,0:T(8,128)(2,1)} %collective-permute-done.29, bf16[256,1024]{1,0:T(8,128)(2,1)} %convert_element_type.330), kind=kOutput, calls=%fused_computation.397 | convolution fusion | flops 2162161664 | bytes 11550720 | tf_op jit(solution)/shard_map/dot_general | solution.py:45
  299.4 4.4 convolution_convert_fusion.1
  311.1 5.3 %all-to-all-start.5 = ((f32[32,1,320]{2,1,0:T(1,128)}), f32[32,1,320]{2,1,0:T(1,128)S(1)}, u32[]{:S(2)}, u32[]{:S(2)}) async-start(f32[32,1,320]{2,1,0:T(1,128)} %all_to_all.70), calls=%async_computation.5 | async-start | bytes 98304 | tf_op jit(solution)/shard_map/all_to_all | solution.py:442
  329.4 6.0 %all-to-all-start.2 = ((bf16[256,4,256]{2,0,1:T(8,128)(2,1)}), bf16[256,4,256]{2,0,1:T(8,128)(2,1)S(1)}, u32[]{:S(2)}, u32[]{:S(2)}) async-start(bf16[256,4,256]{2,0,1:T(8,128)(2,1)} %bitcast.537), calls=%async_computation.2 | async-start | bytes 1048576 | tf_op jit(solution)/shard_map/all_to_all | solution.py:402
  367.1 16.2 %attend_backward.1 = bf16[1024,768]{1,0:T(8,128)(2,1)S(1)} custom-call(bf16[1024,768]{1,0:T(8,128)(2,1)S(1)} %copy-done.1, bf16[1024,768]{1,0:T(8,128)(2,1)S(1)} %copy-done.1, bf16[1024,768]{1,0:T(8,128)(2,1)S(1)} %copy-done.1, bf16[1024,256]{1,0:T(8,128)(2,1)S(1)} %get-tuple-element.28.out_ref, f32[4,1024]{1,0:T(4,128)S(1)} %get-tuple-element.32.total_ref, ...), custom_call_target="tpu_custom_call" | custom-call | flops 2684354560 | bytes 4194304 | tf_op jit(solution)/shard_map/attend_backward/pallas_call | solution.py:169
  397.1 4.7 convolution_convert_fusion.3
  403.3 4.7 all-to-all-start.3
  409.7 18.4 %collective-permute-done.72 = bf16[2,32,2048]{2,1,0:T(8,128)(2,1)S(1)} collective-permute-done((bf16[2,32,2048]{2,1,0:T(8,128)(2,1)S(1)}, bf16[2,32,2048]{2,1,0:T(8,128)(2,1)S(1)}, u32[]{:S(2)}, u32[]{:S(2)}) %collective-permute-start.72) | collective-permute-done | bytes 262176 | tf_op jit(solution)/shard_map/ppermute | solution.py:198
  474.3 17.7 %collective-permute-done.68 = bf16[2,32,2048]{2,1,0:T(8,128)(2,1)S(1)} collective-permute-done((bf16[2,32,2048]{2,1,0:T(8,128)(2,1)S(1)}, bf16[2,32,2048]{2,1,0:T(8,128)(2,1)S(1)}, u32[]{:S(2)}, u32[]{:S(2)}) %collective-permute-start.68) | collective-permute-done | bytes 262176 | tf_op jit(solution)/shard_map/ppermute | solution.py:198
  498.1 4.4 convolution_add_fusion.1
  (508 shorter events, 239.4 us)
Async XLA Ops:
  35.2 28.8 %collective-permute-start.6 = (bf16[2,32,2560]{2,1,0:T(8,128)(2,1)S(1)}, bf16[2,32,2560]{2,1,0:T(8,128)(2,1)S(1)}, u32[]{:S(2)}, u32[]{:S(2)}) collective-permute-start(bf16[2,32,2560]{2,1,0:T(8,128)(2,1)S(1)} %maximum_maximum_fusion), channel_id=1, source_target_pairs={{0,2},{1,3},{2,0},{3,1},{4,6},{5,7},{6,4},{7,5},{8,10},{9,11},{10,... | collective-permute-start | bytes 983048 | tf_op jit(solution)/shard_map/ppermute | solution.py:198
  35.5 28.4 %collective-permute-start.7 = (bf16[2,32,2560]{2,1,0:T(8,128)(2,1)S(1)}, bf16[2,32,2560]{2,1,0:T(8,128)(2,1)S(1)}, u32[]{:S(2)}, u32[]{:S(2)}) collective-permute-start(bf16[2,32,2560]{2,1,0:T(8,128)(2,1)S(1)} %maximum_maximum_fusion), channel_id=1, source_target_pairs={{0,1},{1,2},{2,3},{3,0},{4,5},{5,6},{6,7},{7,4},{8,9},{9,10},{10,1... | collective-permute-start | bytes 983048 | tf_op jit(solution)/shard_map/ppermute | solution.py:198
  37.4 30.9 %collective-permute-start.12 = (bf16[2,128,768]{2,1,0:T(8,128)(2,1)S(1)}, bf16[2,128,768]{2,1,0:T(8,128)(2,1)S(1)}, u32[]{:S(2)}, u32[]{:S(2)}) collective-permute-start(bf16[2,128,768]{2,1,0:T(8,128)(2,1)S(1)} %pad_maximum_fusion.20), channel_id=1, source_target_pairs={{0,16},{16,0},{1,17},{17,1},{2,18},{18,2},{3,19},{19,3},{4,20},{20... | collective-permute-start | bytes 1179656 | tf_op jit(solution)/shard_map/ppermute | solution.py:198
  63.9 47.7 %collective-permute-start.9 = (bf16[256,1024]{1,0:T(8,128)(2,1)S(1)}, bf16[256,1024]{1,0:T(8,128)(2,1)S(1)}, u32[]{:S(2)}, u32[]{:S(2)}) collective-permute-start(bf16[256,1024]{1,0:T(8,128)(2,1)S(1)} %copy-done.21), channel_id=1, source_target_pairs={{0,2},{1,3},{2,0},{3,1},{4,6},{5,7},{6,4},{7,5},{8,10},{9,11},{10,... | collective-permute-start | bytes 1572872 | tf_op jit(solution)/shard_map/ppermute | solution.py:198
  65.9 45.8 %collective-permute-start.10 = (bf16[256,1024]{1,0:T(8,128)(2,1)S(1)}, bf16[256,1024]{1,0:T(8,128)(2,1)S(1)}, u32[]{:S(2)}, u32[]{:S(2)}) collective-permute-start(bf16[256,1024]{1,0:T(8,128)(2,1)S(1)} %copy-done.21), channel_id=1, source_target_pairs={{0,1},{1,2},{2,3},{3,0},{4,5},{5,6},{6,7},{7,4},{8,9},{9,10},{10,1... | collective-permute-start | bytes 1572872 | tf_op jit(solution)/shard_map/ppermute | solution.py:198
  68.5 66.7 %collective-permute-start.13 = (bf16[2,2,128,768]{3,2,1,0:T(8,128)(2,1)S(1)}, bf16[2,2,128,768]{3,2,1,0:T(8,128)(2,1)S(1)}, u32[]{:S(2)}, u32[]{:S(2)}) collective-permute-start(bf16[2,2,128,768]{3,2,1,0:T(8,128)(2,1)S(1)} %pad_maximum_fusion.11), channel_id=1, source_target_pairs={{0,4},{4,0},{1,5},{5,1},{2,6},{6,2},{3,7},{7,3},{8,12},{12,8},{9,1... | collective-permute-start | bytes 2359304 | tf_op jit(solution)/shard_map/ppermute | solution.py:198
  111.8 23.2 %collective-permute-start.22 = (bf16[2,32,2048]{2,1,0:T(8,128)(2,1)S(1)}, bf16[2,32,2048]{2,1,0:T(8,128)(2,1)S(1)}, u32[]{:S(2)}, u32[]{:S(2)}) collective-permute-start(bf16[2,32,2048]{2,1,0:T(8,128)(2,1)S(1)} %pad_maximum_fusion.21), channel_id=1, source_target_pairs={{0,2},{1,3},{2,0},{3,1},{4,6},{5,7},{6,4},{7,5},{8,10},{9,11},{10,... | collective-permute-start | bytes 786440 | tf_op jit(solution)/shard_map/ppermute | solution.py:198
  136.4 27.4 %collective-permute-start.14 = (bf16[128,2560]{1,0:T(8,128)(2,1)}, bf16[128,2560]{1,0:T(8,128)(2,1)}, u32[]{:S(2)}, u32[]{:S(2)}) collective-permute-start(bf16[128,2560]{1,0:T(8,128)(2,1)} %get-tuple-element.85), channel_id=1, source_target_pairs={{0,8},{8,0},{1,9},{9,1},{2,10},{10,2},{3,11},{11,3},{4,12},{12,4},... | collective-permute-start | bytes 1966088 | tf_op jit(solution)/shard_map/ppermute | solution.py:198
  138.3 25.5 %collective-permute-start.16 = (bf16[128,2560]{1,0:T(8,128)(2,1)S(1)}, bf16[128,2560]{1,0:T(8,128)(2,1)}, u32[]{:S(2)}, u32[]{:S(2)}) collective-permute-start(bf16[128,2560]{1,0:T(8,128)(2,1)S(1)} %get-tuple-element.86), channel_id=1, source_target_pairs={{0,16},{16,0},{1,17},{17,1},{2,18},{18,2},{3,19},{19,3},{4,20},{20... | collective-permute-start | bytes 1966088 | tf_op jit(solution)/shard_map/ppermute | solution.py:198
  166.7 29.9 %collective-permute-start.17 = (bf16[2,128,2560]{2,1,0:T(8,128)(2,1)}, bf16[2,128,2560]{2,1,0:T(8,128)(2,1)}, u32[]{:S(2)}, u32[]{:S(2)}) collective-permute-start(bf16[2,128,2560]{2,1,0:T(8,128)(2,1)} %pad_maximum_fusion.5), channel_id=1, source_target_pairs={{0,8},{8,0},{1,9},{9,1},{2,10},{10,2},{3,11},{11,3},{4,12},{12,4},... | collective-permute-start | bytes 3932168 | tf_op jit(solution)/shard_map/ppermute | solution.py:198
  167.9 30.4 %collective-permute-start.15 = (bf16[2,128,2560]{2,1,0:T(8,128)(2,1)}, bf16[2,128,2560]{2,1,0:T(8,128)(2,1)}, u32[]{:S(2)}, u32[]{:S(2)}) collective-permute-start(bf16[2,128,2560]{2,1,0:T(8,128)(2,1)} %pad_maximum_fusion.4), channel_id=1, source_target_pairs={{0,16},{16,0},{1,17},{17,1},{2,18},{18,2},{3,19},{19,3},{4,20},{20... | collective-permute-start | bytes 3932168 | tf_op jit(solution)/shard_map/ppermute | solution.py:198
  250.9 84.6 %collective-permute-start.49 = (bf16[256,1024]{0,1:T(8,128)(2,1)}, bf16[256,1024]{0,1:T(8,128)(2,1)}, u32[]{:S(2)}, u32[]{:S(2)}) collective-permute-start(bf16[256,1024]{0,1:T(8,128)(2,1)} %bitcast.31), channel_id=1, source_target_pairs={{0,4},{4,0},{1,5},{5,1},{2,6},{6,2},{3,7},{7,3},{8,12},{12,8},{9,1... | collective-permute-start | bytes 1572872 | tf_op jit(solution)/shard_map/ppermute | solution.py:198
  279.1 219.0 %collective-permute-start.39 = (bf16[1024,1536]{1,0:T(8,128)(2,1)}, bf16[1024,1536]{1,0:T(8,128)(2,1)}, u32[]{:S(2)}, u32[]{:S(2)}) collective-permute-start(bf16[1024,1536]{1,0:T(8,128)(2,1)} %bitcast.103), channel_id=1, source_target_pairs={{0,4},{4,0},{1,5},{5,1},{2,6},{6,2},{3,7},{7,3},{8,12},{12,8},{9,1... | collective-permute-start | bytes 9437192 | tf_op jit(solution)/shard_map/ppermute | solution.py:198
  295.7 24.5 %collective-permute-start.61 = (bf16[2,128,2048]{2,1,0:T(8,128)(2,1)}, bf16[2,128,2048]{2,1,0:T(8,128)(2,1)}, u32[]{:S(2)}, u32[]{:S(2)}) collective-permute-start(bf16[2,128,2048]{2,1,0:T(8,128)(2,1)} %select_bitcast_fusion.6), channel_id=1, source_target_pairs={{0,16},{16,0},{1,17},{17,1},{2,18},{18,2},{3,19},{19,3},{4,20},{20... | collective-permute-start | bytes 3145736 | tf_op jit(solution)/shard_map/ppermute | solution.py:198
  298.3 25.9 %collective-permute-start.59 = (bf16[2,128,2048]{2,1,0:T(8,128)(2,1)}, bf16[2,128,2048]{2,1,0:T(8,128)(2,1)}, u32[]{:S(2)}, u32[]{:S(2)}) collective-permute-start(bf16[2,128,2048]{2,1,0:T(8,128)(2,1)} %select_bitcast_fusion.7), channel_id=1, source_target_pairs={{0,8},{8,0},{1,9},{9,1},{2,10},{10,2},{3,11},{11,3},{4,12},{12,4},... | collective-permute-start | bytes 3145736 | tf_op jit(solution)/shard_map/ppermute | solution.py:198
  307.0 28.5 %collective-permute-start.50 = (bf16[256,512]{1,0:T(8,128)(2,1)S(1)}, bf16[256,512]{1,0:T(8,128)(2,1)}, u32[]{:S(2)}, u32[]{:S(2)}) collective-permute-start(bf16[256,512]{1,0:T(8,128)(2,1)S(1)} %get-tuple-element.98), channel_id=1, source_target_pairs={{0,4},{4,0},{1,5},{5,1},{2,6},{6,2},{3,7},{7,3},{8,12},{12,8},{9,1... | collective-permute-start | bytes 786440 | tf_op jit(solution)/shard_map/ppermute | solution.py:198
  323.4 25.5 %collective-permute-start.62 = (bf16[128,2048]{1,0:T(8,128)(2,1)}, bf16[128,2048]{1,0:T(8,128)(2,1)S(1)}, u32[]{:S(2)}, u32[]{:S(2)}) collective-permute-start(bf16[128,2048]{1,0:T(8,128)(2,1)} %select_bitcast_fusion.24), channel_id=1, source_target_pairs={{0,8},{8,0},{1,9},{9,1},{2,10},{10,2},{3,11},{11,3},{4,12},{12,4},... | collective-permute-start | bytes 1572872 | tf_op jit(solution)/shard_map/ppermute | solution.py:198
  329.4 36.3 %all-to-all-start.2 = ((bf16[256,4,256]{2,0,1:T(8,128)(2,1)}), bf16[256,4,256]{2,0,1:T(8,128)(2,1)S(1)}, u32[]{:S(2)}, u32[]{:S(2)}) async-start(bf16[256,4,256]{2,0,1:T(8,128)(2,1)} %bitcast.537), calls=%async_computation.2 | async-start | bytes 1048576 | tf_op jit(solution)/shard_map/all_to_all | solution.py:402
  363.8 67.9 %collective-permute-start.63 = (bf16[2,128,2048]{2,1,0:T(8,128)(2,1)}, bf16[2,128,2048]{2,1,0:T(8,128)(2,1)}, u32[]{:S(2)}, u32[]{:S(2)}) collective-permute-start(bf16[2,128,2048]{2,1,0:T(8,128)(2,1)} %select_bitcast_fusion.5), channel_id=1, source_target_pairs={{0,8},{8,0},{1,9},{9,1},{2,10},{10,2},{3,11},{11,3},{4,12},{12,4},... | collective-permute-start | bytes 3145736 | tf_op jit(solution)/shard_map/ppermute | solution.py:198
  396.0 32.1 %collective-permute-start.72 = (bf16[2,32,2048]{2,1,0:T(8,128)(2,1)S(1)}, bf16[2,32,2048]{2,1,0:T(8,128)(2,1)S(1)}, u32[]{:S(2)}, u32[]{:S(2)}) collective-permute-start(bf16[2,32,2048]{2,1,0:T(8,128)(2,1)S(1)} %get-tuple-element.94), channel_id=1, source_target_pairs={{0,2},{1,3},{2,0},{3,1},{4,6},{5,7},{6,4},{7,5},{8,10},{9,11},{10,... | collective-permute-start | bytes 786440 | tf_op jit(solution)/shard_map/ppermute | solution.py:198
  396.0 32.1 %collective-permute-start.71 = (bf16[2,32,2048]{2,1,0:T(8,128)(2,1)S(1)}, bf16[2,32,2048]{2,1,0:T(8,128)(2,1)}, u32[]{:S(2)}, u32[]{:S(2)}) collective-permute-start(bf16[2,32,2048]{2,1,0:T(8,128)(2,1)S(1)} %get-tuple-element.92), channel_id=1, source_target_pairs={{0,1},{1,2},{2,3},{3,0},{4,5},{5,6},{6,7},{7,4},{8,9},{9,10},{10,1... | collective-permute-start | bytes 786440 | tf_op jit(solution)/shard_map/ppermute | solution.py:198
  403.3 91.3 %all-to-all-start.3 = ((bf16[4,256,768]{1,2,0:T(8,128)(2,1)}), bf16[4,256,768]{1,2,0:T(8,128)(2,1)}, u32[]{:S(2)}, u32[]{:S(2)}) async-start(bf16[4,256,768]{1,2,0:T(8,128)(2,1)} %copy.297), calls=%async_computation.3 | async-start | bytes 3145728 | tf_op jit(solution)/shard_map/all_to_all | solution.py:408
  408.2 42.4 %collective-permute-start.65 = (bf16[2,128,2048]{2,1,0:T(8,128)(2,1)S(1)}, bf16[2,128,2048]{2,1,0:T(8,128)(2,1)S(1)}, u32[]{:S(2)}, u32[]{:S(2)}) collective-permute-start(bf16[2,128,2048]{2,1,0:T(8,128)(2,1)S(1)} %copy-done.39), channel_id=1, source_target_pairs={{0,16},{16,0},{1,17},{17,1},{2,18},{18,2},{3,19},{19,3},{4,20},{20... | collective-permute-start | bytes 3145736 | tf_op jit(solution)/shard_map/ppermute | solution.py:198
  467.5 24.5 %collective-permute-start.68 = (bf16[2,32,2048]{2,1,0:T(8,128)(2,1)S(1)}, bf16[2,32,2048]{2,1,0:T(8,128)(2,1)S(1)}, u32[]{:S(2)}, u32[]{:S(2)}) collective-permute-start(bf16[2,32,2048]{2,1,0:T(8,128)(2,1)S(1)} %get-tuple-element.96), channel_id=1, source_target_pairs={{0,2},{1,3},{2,0},{3,1},{4,6},{5,7},{6,4},{7,5},{8,10},{9,11},{10,... | collective-permute-start | bytes 786440 | tf_op jit(solution)/shard_map/ppermute | solution.py:198
  (108 other events, 1009.6 us)

commit v2 on v1

--- a/solution.py
+++ b/solution.py
@@ -8,6 +8,7 @@
 from jax.experimental.pallas import tpu as pltpu
 from jax.sharding import Mesh
 from jax.sharding import PartitionSpec as P
+
 
 HD = 64
 EPS = 1e-12
@@ -206,17 +207,30 @@
     return [shift(block, axis, size, size - d) for d in range(1, size)]
 
 
-def in_order(block, others, axis, size, dim):
+def relayed(block, axis, size):
+    me = lax.axis_index(axis)
+    up, down = [block], [block]
+    for step in range(1, size):
+        up.append(lax.ppermute(up[-1], axis, [(i, i + 1) for i in range(step - 1, size - 1)]))
+        down.append(lax.ppermute(down[-1], axis, [(i, i - 1) for i in range(1, size - step + 1)]))
+    return [jnp.where(me + d < size, down[d], up[size - d]) for d in range(1, size)]
+
+
+def ordered(block, others, axis, size):
     if size == 1:
-        return jnp.expand_dims(block, dim)
+        return [block]
+    ahead = [block] + list(others)
     me = lax.axis_index(axis)
     if size == 2:
-        low = jnp.where(me == 0, block, others[0])
-        high = jnp.where(me == 0, others[0], block)
-        return jnp.stack([low, high], dim)
-    ahead = [block] + list(others)
-    twice = jnp.stack(ahead + ahead, dim)
-    return lax.dynamic_slice_in_dim(twice, lax.rem(size - me, size), size, dim)
+        return [jnp.where(me == 0, *ahead), jnp.where(me == 0, *ahead[::-1])]
+    return [
+        lax.select_n(me, *[ahead[(place - at) % size] for at in range(size)])
+        for place in range(size)
+    ]
+
+
+def in_order(block, others, axis, size, dim):
+    return jnp.stack(ordered(block, others, axis, size), dim)
 
 
 def gather_blocks(block, axis, size, dim):
@@ -302,17 +316,23 @@
         high = jnp.where(core_at == 0, came, kept)
         return jnp.concatenate([low, high], 1)
 
-    small = (b_query, b_value, b_out, ln1_gain, ln1_shift, b_up, b_down, ln2_gain, ln2_shift)
-    packed = jnp.concatenate(small)[None]
-    packed = lax.all_to_all(
-        jnp.tile(packed, (devices, 1)), ALL, split_axis=0, concat_axis=0, tiled=True
-    ).astype(F32)
-    vectors, place = [], 0
-    for shard in small:
-        vectors.append(packed[:, place : place + shard.shape[0]].reshape(-1))
-        place += shard.shape[0]
-    (bias_query, bias_value, bias_out, gain_one, shift_one, bias_up, bias_down, gain_two,
-     shift_two) = vectors
+    def to_owners(matrix, kept, count):
+        came = [
+            shift(matrix[d * count : (d + 1) * count], "seq", ns, d) for d in range(1, ns)
+        ]
+        return jnp.concatenate(ordered(kept, came[::-1], "seq", ns), 1)
+
+    def to_heads(matrix):
+        columns = matrix.shape[1] // ns
+
+        def block(d):
+            return lax.dynamic_slice_in_dim(
+                matrix, lax.rem(seq_at + d, ns) * columns, columns, 1
+            )
+
+        sent = [block(d) for d in range(1, ns)]
+        came = [shift(part, "seq", ns, d) for d, part in enumerate(sent, 1)]
+        return jnp.concatenate([block(0)] + came[::-1], 0)
 
     by_owner = w_qkv.reshape(rows, 3, ns, own).transpose(0, 2, 1, 3).reshape(rows, 3 * width)
     to_owner = by_owner.reshape(rows, ns, 3 * own)
@@ -328,19 +348,31 @@
     plane = gather_blocks(gather_blocks(own_line, "x", nx, 0), "y", ny, 0)
     own_qkv = gather_blocks(plane, "core", nc, 2).reshape(width, 3 * own)
 
+    small = (b_query, b_value, b_out, ln1_gain, ln1_shift, b_up, b_down, ln2_gain, ln2_shift)
+    packed = jnp.concatenate((after(small[0], *came),) + small[1:])[None]
+    packed = lax.all_to_all(
+        jnp.tile(packed, (devices, 1)), ALL, split_axis=0, concat_axis=0, tiled=True
+    ).astype(F32)
+    vectors, place = [], 0
+    for shard in small:
+        vectors.append(packed[:, place : place + shard.shape[0]].reshape(-1))
+        place += shard.shape[0]
+    (bias_query, bias_value, bias_out, gain_one, shift_one, bias_up, bias_down, gain_two,
+     shift_two) = vectors
+
     up_out = own_columns(w_up), own_columns(w_out)
     up_out = after(jnp.concatenate(up_out, 2), *came)
     up_line = shifts(up_out, "seq", ns)
     hidden_sent = after(hidden_states, *up_line)
-    hidden_line = shifts(hidden_sent, "seq", ns)
-    seq_hidden = in_order(hidden_sent, hidden_line, "seq", ns, 0).reshape(ns * tokens, width)
+    hidden_line = relayed(hidden_sent, "seq", ns)
+    seq_hidden = jnp.concatenate([hidden_sent] + hidden_line, 0)
     down_own = after(own_columns(w_down), *hidden_line)
     down_line = shifts(down_own, "seq", ns)
-    half_up_out = plane_of(after(line_of(up_out, up_line), own_qkv))
+    half_up_out = plane_of(line_of(up_out, up_line))
     half = inner_width // nc
     half_up, half_out = half_up_out[:, :half], half_up_out[:, half:]
     other_out = swap(half_out)
-    half_down = plane_of(after(line_of(down_own, down_line), half_up_out))
+    half_down = plane_of(line_of(down_own, down_line))
 
     own_bias = jnp.concatenate(
         [
@@ -351,7 +383,7 @@
     )
     projected = (dot(seq_hidden, own_qkv) + own_bias).astype(BF16)
     outputs, log_total = attend_forward(projected)
-    attn_tok = lax.all_to_all(outputs, "seq", split_axis=0, concat_axis=1, tiled=True)
+    attn_tok = to_owners(outputs, outputs[:tokens], tokens)
     qkv_own = after(own_columns(by_owner), attn_tok)
     qkv_line = shifts(qkv_own, "seq", ns)
     half_qkv = plane_of(after(line_of(qkv_own, qkv_line), half_down))
@@ -370,7 +402,8 @@
     hidden_low = hidden_one.astype(BF16)
 
     hidden_two = pair(hidden_low)
-    gelu_value, gelu_slope = gelu_both(dot(hidden_two, half_up) + halves(bias_up)[0])
+    inner = dot(hidden_two, half_up)
+    gelu_value, gelu_slope = gelu_both(inner + halves(bias_up)[0])
     active_low = gelu_value.astype(BF16)
     resid_two = hidden_one + own_tokens(contract_last(active_low, half_down))
     layer_val, normed_two, inv_two = layer_norm(resid_two + bias_down, gain_two, shift_two)
@@ -384,12 +417,13 @@
     grad_bias_down = jnp.sum(grad_resid_two, 0)
     sum_down = contract_first(grad_low_two, active_low).astype(BF16)
     sum_down = over_plane(sum_down)
-    grad_inner = dot(grad_low_two, half_down) * gelu_slope
+    grad_inner = dot(grad_low_two, half_down)
+    grad_inner = grad_inner * gelu_slope
     grad_inner_low = grad_inner.astype(BF16)
     grad_bias_up = jnp.sum(grad_inner, 0)
     grad_hidden = grad_resid_two + own_tokens(contract_last(grad_inner_low, half_up))
     sum_up = contract_first(hidden_two, grad_inner_low).astype(BF16)
-    sum_up = over_plane(after(sum_up, sum_down))
+    sum_up = over_plane(sum_up)
     grad_gain_one = jnp.sum(grad_hidden * normed_one, 0)
     grad_shift_one = jnp.sum(grad_hidden, 0)
     grad_resid_one = norm_back(grad_hidden, normed_one, inv_one, gain_one)
@@ -399,13 +433,13 @@
     grad_attn = (
         contract_last(grad_kept, half_out) + contract_last(grad_sent, other_out)
     ).astype(BF16)
-    grad_attn_cols = lax.all_to_all(grad_attn, "seq", split_axis=1, concat_axis=0, tiled=True)
+    grad_attn_cols = to_heads(grad_attn)
     grad_out_two = jnp.concatenate([grad_kept, swap(grad_sent)], 0)
     sum_out = contract_first(pair(attn_tok), grad_out_two).astype(BF16)
-    sum_out = over_plane(after(sum_out, sum_up))
+    sum_out = over_plane(sum_out)
 
     grad_own = attend_backward(projected, outputs, log_total, grad_attn_cols)
-    grad_tok = lax.all_to_all(grad_own, "seq", split_axis=0, concat_axis=1, tiled=True)
+    grad_tok = to_owners(grad_own, grad_own[:tokens], tokens)
     own_kept, own_sent = halves(grad_own)
     other_sum = swap(contract_first(seq_hidden, own_sent).astype(BF16))
     sum_qkv = (contract_first(seq_hidden, own_kept) + other_sum.astype(F32)).astype(BF16)
@@ -426,7 +460,9 @@
     sum_qkv = sum_qkv.reshape(rows, 3 * width)
     tok_kept, tok_other = halves(grad_tok)
     grad_input = (
-        grad_resid_one + contract_last(tok_kept, half_qkv) + contract_last(tok_other, other_qkv)
+        grad_resid_one
+        + contract_last(tok_kept, half_qkv)
+        + contract_last(tok_other, other_qkv)
     )
     sum_down = over_line(after(sum_down, grad_attn_cols))
     sum_up = over_line(sum_up)
@@ -439,7 +475,7 @@
 
     def sum_small(parts):
         stacked = jnp.concatenate([part.reshape(devices, -1) for part in parts], 1)
-        arrived = lax.all_to_all(stacked, ALL, split_axis=0, concat_axis=0, tiled=True)
+        arrived = lax.all_to_all(after(stacked, grad_tok), ALL, split_axis=0, concat_axis=0, tiled=True)
         total = jnp.sum(arrived, 0)
         ends, place = [], 0
         for part in parts:
@@ -449,13 +485,10 @@
         return ends
 
     (sum_gain_two, sum_shift_two, sum_bias_down, sum_bias_up, sum_gain_one, sum_shift_one,
-     sum_bias_out) = sum_small(
+     sum_bias_out, sum_bias_query, sum_bias_value) = sum_small(
         (grad_gain_two, grad_shift_two, grad_bias_down,
          spread(grad_bias_up, inner_width, core_at * half), grad_gain_one, grad_shift_one,
-         grad_bias_out)
-    )
-    sum_bias_query, sum_bias_value = sum_small(
-        (spread(own_sums[:own], width, seq_at * own),
+         grad_bias_out, spread(own_sums[:own], width, seq_at * own),
          spread(own_sums[2 * own :], width, seq_at * own))
     )
     return (layer_out, grad_input, sum_qkv, sum_bias_query, sum_bias_value, sum_out, sum_bias_out,

time: 513 us -> 517 us (level)
  starting transfers between devices: 96.9 us -> 144 us
  waiting for transfers between devices: 230 us -> 194 us
  local copies, waits for them, and re-layouts: 48.1 us -> 37.7 us
  other arithmetic: 48.1 us -> 53.5 us
    ppermute x75 -> x81, waiting for transfers between devices: 220 us -> 161 us  [shift(): lax.ppermute(block, axis, [(i, (i + distance) % size) for i in range(size)])]
    ppermute x75 -> x81, starting transfers between devices: 66.9 us -> 121 us  [shift(): lax.ppermute(block, axis, [(i, (i + distance) % size) for i in range(size)])]
    ppermute x0 -> x6, waiting for transfers between devices: none -> 27.3 us  [the longest x3 27.3 us: relayed(): lax.ppermute(down[-1], axis, [(i, i - 1) for i in range(1, size - step +...]
    all_to_all x5 -> x1, starting transfers between devices: 22.7 us -> 2.81 us  [sum_small(): lax.all_to_all(after(stacked, grad_tok), ALL, split_axis=0, concat_axis=0...]
    ppermute x0 -> x6, starting transfers between devices: none -> 15.1 us  [the longest x3 11.3 us: relayed(): lax.ppermute(up[-1], axis, [(i, i + 1) for i in range(step - 1, size - 1)])]
    all_to_all x5 -> x1, waiting for transfers between devices: 9.7 us -> 0.01 us  [sum_small(): lax.all_to_all(after(stacked, grad_tok), ALL, split_axis=0, concat_axis=0...]
    concatenate x1, local copies, waits for them, and re-layouts: 6.1 us -> 0.11 us  [body(): packed = jnp.concatenate((after(small[0], *came),) + small[1:])[None]]
    all_to_all x1, waiting for transfers between devices: 0.01 us -> 5.39 us  [body(): lax.all_to_all(jnp.tile(packed, (devices, 1)), ALL, split_axis=0, concat_...]
  transfers between devices with their start and end apart: 81 -> 89, of which waited for: 37 -> 33; matrix products, arithmetic and copies ran while one was open for 22% -> 23% of each run, Pallas kernels for 6% -> 6%
where the time goes in v2:
time: 517 us; the launch traced here: 508 us
  waiting for transfers between devices  194 us (38%)
  starting transfers between devices  144 us (28%)
  other arithmetic  53.5 us (10%)
  matrix products  43.5 us (8%)
  local copies, waits for them, and re-layouts  37.7 us (7%)
  Pallas kernels  32.1 us (6%)
    ppermute x81, waiting for transfers between devices, shift(): lax.ppermute(block, axis, [(i, (i + distance) % size) for i in range(size)])  161 us
    ppermute x81, starting transfers between devices, shift(): lax.ppermute(block, axis, [(i, (i + distance) % size) for i in range(size)])  121 us
    ppermute x3, waiting for transfers between devices, relayed(): lax.ppermute(down[-1], axis, [(i, i - 1) for i in range(1, size - step +...  27.3 us
    dot_general x6, matrix products, contract_last(): lax.dot_general(left, right, (((1,), (1,)), ((), ())), preferred_element_...  16.6 us
    pallas_call x1, Pallas kernels, attend_backward(): pl.pallas_call(functools.partial(backward_kernel, 1.0 / math.sqrt(HD), bl...  16.2 us
    pallas_call x1, Pallas kernels, attend_forward(): pl.pallas_call(functools.partial(forward_kernel, 1.0 / math.sqrt(HD)), gr...  15.9 us
    dot_general x5, matrix products, contract_first(): lax.dot_general(left, right, (((0,), (0,)), ((), ())), preferred_element_...  15.1 us
    select_n x22, other arithmetic, pick(): return jnp.where(index == 0, first, second)  12.2 us
  transfers between devices with their start and end apart: 89, of which 33 were waited for; matrix products, arithmetic and copies ran while one was open for 23% of the time, Pallas kernels for 6%

profile of v2, /device:TPU:0, one launch (start us, length us, event | category | flops | bytes accessed | tf_op | source)
XLA Modules:
  0.0 507.7 jit_solution(8386185413369044895)
XLA Ops:
  32.6 14.9 %collective-permute-done.6 = bf16[2,32,2560]{2,1,0:T(8,128)(2,1)S(1)} collective-permute-done((bf16[2,32,2560]{2,1,0:T(8,128)(2,1)S(1)}, bf16[2,32,2560]{2,1,0:T(8,128)(2,1)S(1)}, u32[]{:S(2)}, u32[]{:S(2)}) %collective-permute-start.6) | collective-permute-done | bytes 327712 | tf_op jit(solution)/shard_map/ppermute | solution.py:199
  47.5 6.2 %collective-permute-done.7 = bf16[2,32,2560]{2,1,0:T(8,128)(2,1)S(1)} collective-permute-done((bf16[2,32,2560]{2,1,0:T(8,128)(2,1)S(1)}, bf16[2,32,2560]{2,1,0:T(8,128)(2,1)S(1)}, u32[]{:S(2)}, u32[]{:S(2)}) %collective-permute-start.7) | collective-permute-done | bytes 327712 | tf_op jit(solution)/shard_map/ppermute | solution.py:199
  56.4 9.9 %collective-permute-start.9 = (bf16[256,1024]{1,0:T(8,128)(2,1)S(1)}, bf16[256,1024]{1,0:T(8,128)(2,1)S(1)}, u32[]{:S(2)}, u32[]{:S(2)}) collective-permute-start(bf16[256,1024]{1,0:T(8,128)(2,1)S(1)} %copy-done.41), channel_id=1, source_target_pairs={{0,1},{1,2},{2,3},{4,5},{5,6},{6,7},{8,9},{9,10},{10,11},{12,13},{... | collective-permute-start | bytes 1572872 | tf_op jit(solution)/shard_map/ppermute | solution.py:214
  67.3 8.8 %collective-permute-done.8 = bf16[256,1024]{1,0:T(8,128)(2,1)S(1)} collective-permute-done((bf16[256,1024]{1,0:T(8,128)(2,1)S(1)}, bf16[256,1024]{1,0:T(8,128)(2,1)S(1)}, u32[]{:S(2)}, u32[]{:S(2)}) %collective-permute-start.8) | collective-permute-done | bytes 524320 | tf_op jit(solution)/shard_map/ppermute | solution.py:215
  84.1 6.9 %collective-permute-done.12 = bf16[256,1024]{1,0:T(8,128)(2,1)S(1)} collective-permute-done((bf16[256,1024]{1,0:T(8,128)(2,1)S(1)}, bf16[256,1024]{1,0:T(8,128)(2,1)S(1)}, u32[]{:S(2)}, u32[]{:S(2)}) %collective-permute-start.12) | collective-permute-done | bytes 524320 | tf_op jit(solution)/shard_map/ppermute | solution.py:215
  93.4 11.6 %collective-permute-done.13 = bf16[256,1024]{1,0:T(8,128)(2,1)S(1)} collective-permute-done((bf16[256,1024]{1,0:T(8,128)(2,1)S(1)}, bf16[256,1024]{1,0:T(8,128)(2,1)S(1)}, u32[]{:S(2)}, u32[]{:S(2)}) %collective-permute-start.13) | collective-permute-done | bytes 524320 | tf_op jit(solution)/shard_map/ppermute | solution.py:215
  107.9 15.9 %attend_forward.1 = (bf16[1024,256]{1,0:T(8,128)(2,1)S(1)}, f32[4,1024]{1,0:T(4,128)S(1)}) custom-call(bf16[1024,768]{1,0:T(8,128)(2,1)S(1)} %add_convert_fusion.query_ref.key_ref.value_ref, bf16[1024,768]{1,0:T(8,128)(2,1)S(1)} %add_convert_fusion.query_ref.key_ref.value_ref, bf16[1024,768]{1,0:T(8,128)(2,1)S(1)} %add_convert_fusion.query_ref.key_ref.value_ref), custom_call_target="tpu_custom_call" | custom-call | flops 1073741824 | bytes 2097152 | tf_op jit(solution)/shard_map/attend_forward/pallas_call | solution.py:89
  129.3 8.9 %collective-permute-done.18 = bf16[256,256]{1,0:T(8,128)(2,1)S(1)} collective-permute-done((bf16[256,256]{1,0:T(8,128)(2,1)S(1)}, bf16[256,256]{1,0:T(8,128)(2,1)S(1)}, u32[]{:S(2)}, u32[]{:S(2)}) %collective-permute-start.18) | collective-permute-done | bytes 131104 | tf_op jit(solution)/shard_map/ppermute | solution.py:199
  146.3 8.7 %collective-permute-done.28 = bf16[2,32,2048]{2,1,0:T(8,128)(2,1)S(1)} collective-permute-done((bf16[2,32,2048]{2,1,0:T(8,128)(2,1)S(1)}, bf16[2,32,2048]{2,1,0:T(8,128)(2,1)S(1)}, u32[]{:S(2)}, u32[]{:S(2)}) %collective-permute-start.28) | collective-permute-done | bytes 262176 | tf_op jit(solution)/shard_map/ppermute | solution.py:199
  159.1 9.4 %collective-permute-start.44 = (bf16[2,32,1536]{2,1,0:T(8,128)(2,1)S(1)}, bf16[2,32,1536]{2,1,0:T(8,128)(2,1)S(1)}, u32[]{:S(2)}, u32[]{:S(2)}) collective-permute-start(bf16[2,32,1536]{2,1,0:T(8,128)(2,1)S(1)} %pad_maximum_fusion.30), channel_id=1, source_target_pairs={{0,1},{1,2},{2,3},{3,0},{4,5},{5,6},{6,7},{7,4},{8,9},{9,10},{10,1... | collective-permute-start | bytes 589832 | tf_op jit(solution)/shard_map/ppermute | solution.py:199
  189.3 16.7 %collective-permute-done.33 = bf16[2,128,2048]{2,1,0:T(8,128)(2,1)S(1)} collective-permute-done((bf16[2,128,2048]{2,1,0:T(8,128)(2,1)S(1)}, bf16[2,128,2048]{2,1,0:T(8,128)(2,1)S(1)}, u32[]{:S(2)}, u32[]{:S(2)}) %collective-permute-start.33) | collective-permute-done | bytes 1048608 | tf_op jit(solution)/shard_map/ppermute | solution.py:199
  230.9 10.0 %collective-permute-done.50 = bf16[2,128,1536]{2,1,0:T(8,128)(2,1)} collective-permute-done((bf16[2,128,1536]{2,1,0:T(8,128)(2,1)}, bf16[2,128,1536]{2,1,0:T(8,128)(2,1)}, u32[]{:S(2)}, u32[]{:S(2)}) %collective-permute-start.50) | collective-permute-done | bytes 786464 | tf_op jit(solution)/shard_map/ppermute | solution.py:199
  280.0 6.1 %collective-permute-done.71 = bf16[2,128,2048]{2,1,0:T(8,128)(2,1)} collective-permute-done((bf16[2,128,2048]{2,1,0:T(8,128)(2,1)}, bf16[2,128,2048]{2,1,0:T(8,128)(2,1)}, u32[]{:S(2)}, u32[]{:S(2)}) %collective-permute-start.71) | collective-permute-done | bytes 1048608 | tf_op jit(solution)/shard_map/ppermute | solution.py:199
  297.9 12.5 %collective-permute-done.81 = bf16[2,128,2048]{2,1,0:T(8,128)(2,1)} collective-permute-done((bf16[2,128,2048]{2,1,0:T(8,128)(2,1)}, bf16[2,128,2048]{2,1,0:T(8,128)(2,1)}, u32[]{:S(2)}, u32[]{:S(2)}) %collective-permute-start.81) | collective-permute-done | bytes 1048608 | tf_op jit(solution)/shard_map/ppermute | solution.py:199
  314.8 5.5 %collective-permute-start.37 = (bf16[256,256]{1,0:T(8,128)(2,1)S(1)}, bf16[256,256]{1,0:T(8,128)(2,1)S(1)}, u32[]{:S(2)}, u32[]{:S(2)}) collective-permute-start(bf16[256,256]{1,0:T(8,128)(2,1)S(1)} %get-tuple-element.138), channel_id=1, source_target_pairs={{0,3},{1,0},{2,1},{3,2},{4,7},{5,4},{6,5},{7,6},{8,11},{9,8},{10,9... | collective-permute-start | bytes 393224 | tf_op jit(solution)/shard_map/ppermute | solution.py:199
  325.5 16.2 %attend_backward.1 = bf16[1024,768]{1,0:T(8,128)(2,1)S(1)} custom-call(bf16[1024,768]{1,0:T(8,128)(2,1)S(1)} %copy-done.1, bf16[1024,768]{1,0:T(8,128)(2,1)S(1)} %copy-done.1, bf16[1024,768]{1,0:T(8,128)(2,1)S(1)} %copy-done.1, bf16[1024,256]{1,0:T(8,128)(2,1)S(1)} %get-tuple-element.28.out_ref, f32[4,1024]{1,0:T(4,128)S(1)} %get-tuple-element.30.total_ref, ...), custom_call_target="tpu_custom_call" | custom-call | flops 2684354560 | bytes 4194304 | tf_op jit(solution)/shard_map/attend_backward/pallas_call | solution.py:170
  362.9 15.6 %collective-permute-done.42 = bf16[256,768]{1,0:T(8,128)(2,1)S(1)} collective-permute-done((bf16[256,768]{1,0:T(8,128)(2,1)S(1)}, bf16[256,768]{1,0:T(8,128)(2,1)S(1)}, u32[]{:S(2)}, u32[]{:S(2)}) %collective-permute-start.42) | collective-permute-done | bytes 393248 | tf_op jit(solution)/shard_map/ppermute | solution.py:199
  404.4 6.3 %collective-permute-done.65 = bf16[2,128,512]{2,1,0:T(8,128)(2,1)S(1)} collective-permute-done((bf16[2,128,512]{2,1,0:T(8,128)(2,1)S(1)}, bf16[2,128,512]{2,1,0:T(8,128)(2,1)S(1)}, u32[]{:S(2)}, u32[]{:S(2)}) %collective-permute-start.65) | collective-permute-done | bytes 262176 | tf_op jit(solution)/shard_map/ppermute | solution.py:199
  418.2 6.0 %collective-permute-start.69 = (bf16[2,32,512]{2,1,0:T(8,128)(2,1)}, bf16[2,32,512]{2,1,0:T(8,128)(2,1)}, u32[]{:S(2)}, u32[]{:S(2)}) collective-permute-start(bf16[2,32,512]{2,1,0:T(8,128)(2,1)} %get-tuple-element.164), channel_id=1, source_target_pairs={{0,3},{1,0},{2,1},{3,2},{4,7},{5,4},{6,5},{7,6},{8,11},{9,8},{10,9... | collective-permute-start | bytes 196616 | tf_op jit(solution)/shard_map/ppermute | solution.py:199
  433.3 10.3 %collective-permute-start.75 = (bf16[2,32,2048]{2,1,0:T(8,128)(2,1)S(1)}, bf16[2,32,2048]{2,1,0:T(8,128)(2,1)S(1)}, u32[]{:S(2)}, u32[]{:S(2)}) collective-permute-start(bf16[2,32,2048]{2,1,0:T(8,128)(2,1)S(1)} %get-tuple-element.100), channel_id=1, source_target_pairs={{0,1},{1,2},{2,3},{3,0},{4,5},{5,6},{6,7},{7,4},{8,9},{9,10},{10,1... | collective-permute-start | bytes 786440 | tf_op jit(solution)/shard_map/ppermute | solution.py:199
  444.3 12.2 %collective-permute-done.76 = bf16[2,32,2048]{2,1,0:T(8,128)(2,1)S(1)} collective-permute-done((bf16[2,32,2048]{2,1,0:T(8,128)(2,1)}, bf16[2,32,2048]{2,1,0:T(8,128)(2,1)S(1)}, u32[]{:S(2)}, u32[]{:S(2)}) %collective-permute-start.76) | collective-permute-done | bytes 262176 | tf_op jit(solution)/shard_map/ppermute | solution.py:199
  456.5 7.7 %collective-permute-start.83 = (bf16[2,32,2048]{2,1,0:T(8,128)(2,1)S(1)}, bf16[2,32,2048]{2,1,0:T(8,128)(2,1)S(1)}, u32[]{:S(2)}, u32[]{:S(2)}) collective-permute-start(bf16[2,32,2048]{2,1,0:T(8,128)(2,1)S(1)} %get-tuple-element.97), channel_id=1, source_target_pairs={{0,1},{1,2},{2,3},{3,0},{4,5},{5,6},{6,7},{7,4},{8,9},{9,10},{10,1... | collective-permute-start | bytes 786440 | tf_op jit(solution)/shard_map/ppermute | solution.py:199
  464.4 9.9 %collective-permute-done.84 = bf16[2,32,2048]{2,1,0:T(8,128)(2,1)S(1)} collective-permute-done((bf16[2,32,2048]{2,1,0:T(8,128)(2,1)S(1)}, bf16[2,32,2048]{2,1,0:T(8,128)(2,1)S(1)}, u32[]{:S(2)}, u32[]{:S(2)}) %collective-permute-start.84) | collective-permute-done | bytes 262176 | tf_op jit(solution)/shard_map/ppermute | solution.py:199
  478.7 5.8 %collective-permute-done.55 = bf16[2,128,384]{2,1,0:T(8,128)(2,1)S(1)} collective-permute-done((bf16[2,128,384]{2,1,0:T(8,128)(2,1)S(1)}, bf16[2,128,384]{2,1,0:T(8,128)(2,1)S(1)}, u32[]{:S(2)}, u32[]{:S(2)}) %collective-permute-start.55) | collective-permute-done | bytes 196640 | tf_op jit(solution)/shard_map/ppermute | solution.py:199
  (581 shorter events, 262.2 us)
Async XLA Ops:
  12.7 42.2 %collective-permute-start.26 = (bf16[32,2048]{1,0:T(8,128)(2,1)S(1)}, bf16[32,2048]{1,0:T(8,128)(2,1)S(1)}, u32[]{:S(2)}, u32[]{:S(2)}) collective-permute-start(bf16[32,2048]{1,0:T(8,128)(2,1)S(1)} %bitcast.546), channel_id=1, source_target_pairs={{0,4},{4,0},{1,5},{5,1},{2,6},{6,2},{3,7},{7,3},{8,12},{12,8},{9,1... | collective-permute-start | bytes 393224 | tf_op jit(solution)/shard_map/ppermute | solution.py:199
  31.8 21.9 %collective-permute-start.7 = (bf16[2,32,2560]{2,1,0:T(8,128)(2,1)S(1)}, bf16[2,32,2560]{2,1,0:T(8,128)(2,1)S(1)}, u32[]{:S(2)}, u32[]{:S(2)}) collective-permute-start(bf16[2,32,2560]{2,1,0:T(8,128)(2,1)S(1)} %maximum_maximum_fusion), channel_id=1, source_target_pairs={{0,1},{1,2},{2,3},{3,0},{4,5},{5,6},{6,7},{7,4},{8,9},{9,10},{10,1... | collective-permute-start | bytes 983048 | tf_op jit(solution)/shard_map/ppermute | solution.py:199
  31.9 35.2 %collective-permute-start.15 = (bf16[2,128,768]{2,1,0:T(8,128)(2,1)S(1)}, bf16[2,128,768]{2,1,0:T(8,128)(2,1)S(1)}, u32[]{:S(2)}, u32[]{:S(2)}) collective-permute-start(bf16[2,128,768]{2,1,0:T(8,128)(2,1)S(1)} %pad_maximum_fusion.27), channel_id=1, source_target_pairs={{0,16},{16,0},{1,17},{17,1},{2,18},{18,2},{3,19},{19,3},{4,20},{20... | collective-permute-start | bytes 1179656 | tf_op jit(solution)/shard_map/ppermute | solution.py:199
  54.2 24.0 %collective-permute-start.22 = (bf16[128,2560]{1,0:T(8,128)(2,1)S(1)}, bf16[128,2560]{1,0:T(8,128)(2,1)S(1)}, u32[]{:S(2)}, u32[]{:S(2)}) collective-permute-start(bf16[128,2560]{1,0:T(8,128)(2,1)S(1)} %bitcast.527), channel_id=1, source_target_pairs={{0,16},{16,0},{1,17},{17,1},{2,18},{18,2},{3,19},{19,3},{4,20},{20... | collective-permute-start | bytes 1966088 | tf_op jit(solution)/shard_map/ppermute | solution.py:199
  67.3 25.0 %collective-permute-start.16 = (bf16[2,2,128,768]{3,2,1,0:T(8,128)(2,1)S(1)}, bf16[2,2,128,768]{3,2,1,0:T(8,128)(2,1)S(1)}, u32[]{:S(2)}, u32[]{:S(2)}) collective-permute-start(bf16[2,2,128,768]{3,2,1,0:T(8,128)(2,1)S(1)} %pad_maximum_fusion.15), channel_id=1, source_target_pairs={{0,4},{4,0},{1,5},{5,1},{2,6},{6,2},{3,7},{7,3},{8,12},{12,8},{9,1... | collective-permute-start | bytes 2359304 | tf_op jit(solution)/shard_map/ppermute | solution.py:199
  78.4 97.8 %collective-permute-start.23 = (bf16[2,128,2560]{2,1,0:T(8,128)(2,1)S(1)}, bf16[2,128,2560]{2,1,0:T(8,128)(2,1)S(1)}, u32[]{:S(2)}, u32[]{:S(2)}) collective-permute-start(bf16[2,128,2560]{2,1,0:T(8,128)(2,1)S(1)} %pad_maximum_fusion.8), channel_id=1, source_target_pairs={{0,8},{8,0},{1,9},{9,1},{2,10},{10,2},{3,11},{11,3},{4,12},{12,4},... | collective-permute-start | bytes 3932168 | tf_op jit(solution)/shard_map/ppermute | solution.py:199
  128.4 48.2 %collective-permute-start.21 = (bf16[2,128,2560]{2,1,0:T(8,128)(2,1)S(1)}, bf16[2,128,2560]{2,1,0:T(8,128)(2,1)S(1)}, u32[]{:S(2)}, u32[]{:S(2)}) collective-permute-start(bf16[2,128,2560]{2,1,0:T(8,128)(2,1)S(1)} %pad_maximum_fusion.7), channel_id=1, source_target_pairs={{0,16},{16,0},{1,17},{17,1},{2,18},{18,2},{3,19},{19,3},{4,20},{20... | collective-permute-start | bytes 3932168 | tf_op jit(solution)/shard_map/ppermute | solution.py:199
  180.8 25.2 %collective-permute-start.33 = (bf16[2,128,2048]{2,1,0:T(8,128)(2,1)S(1)}, bf16[2,128,2048]{2,1,0:T(8,128)(2,1)S(1)}, u32[]{:S(2)}, u32[]{:S(2)}) collective-permute-start(bf16[2,128,2048]{2,1,0:T(8,128)(2,1)S(1)} %pad_maximum_fusion.12), channel_id=1, source_target_pairs={{0,8},{8,0},{1,9},{9,1},{2,10},{10,2},{3,11},{11,3},{4,12},{12,4},... | collective-permute-start | bytes 3145736 | tf_op jit(solution)/shard_map/ppermute | solution.py:199
  218.3 134.8 %collective-permute-start.61 = (bf16[256,1024]{1,0:T(8,128)(2,1)}, bf16[256,1024]{1,0:T(8,128)(2,1)}, u32[]{:S(2)}, u32[]{:S(2)}) collective-permute-start(bf16[256,1024]{1,0:T(8,128)(2,1)} %pad_maximum_fusion.23), channel_id=1, source_target_pairs={{0,4},{4,0},{1,5},{5,1},{2,6},{6,2},{3,7},{7,3},{8,12},{12,8},{9,1... | collective-permute-start | bytes 1572872 | tf_op jit(solution)/shard_map/ppermute | solution.py:199
  246.1 257.0 %collective-permute-start.51 = (bf16[1024,1536]{1,0:T(8,128)(2,1)}, bf16[1024,1536]{1,0:T(8,128)(2,1)}, u32[]{:S(2)}, u32[]{:S(2)}) collective-permute-start(bf16[1024,1536]{1,0:T(8,128)(2,1)} %bitcast.87), channel_id=1, source_target_pairs={{0,4},{4,0},{1,5},{5,1},{2,6},{6,2},{3,7},{7,3},{8,12},{12,8},{9,1... | collective-permute-start | bytes 9437192 | tf_op jit(solution)/shard_map/ppermute | solution.py:199
  261.2 24.9 %collective-permute-start.71 = (bf16[2,128,2048]{2,1,0:T(8,128)(2,1)}, bf16[2,128,2048]{2,1,0:T(8,128)(2,1)}, u32[]{:S(2)}, u32[]{:S(2)}) collective-permute-start(bf16[2,128,2048]{2,1,0:T(8,128)(2,1)} %select_bitcast_fusion.7), channel_id=1, source_target_pairs={{0,8},{8,0},{1,9},{9,1},{2,10},{10,2},{3,11},{11,3},{4,12},{12,4},... | collective-permute-start | bytes 3145736 | tf_op jit(solution)/shard_map/ppermute | solution.py:199
  263.4 26.8 %collective-permute-start.73 = (bf16[2,128,2048]{2,1,0:T(8,128)(2,1)}, bf16[2,128,2048]{2,1,0:T(8,128)(2,1)}, u32[]{:S(2)}, u32[]{:S(2)}) collective-permute-start(bf16[2,128,2048]{2,1,0:T(8,128)(2,1)} %select_bitcast_fusion.6), channel_id=1, source_target_pairs={{0,16},{16,0},{1,17},{17,1},{2,18},{18,2},{3,19},{19,3},{4,20},{20... | collective-permute-start | bytes 3145736 | tf_op jit(solution)/shard_map/ppermute | solution.py:199
  272.1 38.3 %collective-permute-start.81 = (bf16[2,128,2048]{2,1,0:T(8,128)(2,1)}, bf16[2,128,2048]{2,1,0:T(8,128)(2,1)}, u32[]{:S(2)}, u32[]{:S(2)}) collective-permute-start(bf16[2,128,2048]{2,1,0:T(8,128)(2,1)} %select_bitcast_fusion.4), channel_id=1, source_target_pairs={{0,16},{16,0},{1,17},{17,1},{2,18},{18,2},{3,19},{19,3},{4,20},{20... | collective-permute-start | bytes 3145736 | tf_op jit(solution)/shard_map/ppermute | solution.py:199
  286.1 28.7 %collective-permute-start.79 = (bf16[2,128,2048]{2,1,0:T(8,128)(2,1)S(1)}, bf16[2,128,2048]{2,1,0:T(8,128)(2,1)S(1)}, u32[]{:S(2)}, u32[]{:S(2)}) collective-permute-start(bf16[2,128,2048]{2,1,0:T(8,128)(2,1)S(1)} %copy-done.37), channel_id=1, source_target_pairs={{0,8},{8,0},{1,9},{9,1},{2,10},{10,2},{3,11},{11,3},{4,12},{12,4},... | collective-permute-start | bytes 3145736 | tf_op jit(solution)/shard_map/ppermute | solution.py:199
  290.2 32.0 %collective-permute-start.39 = (bf16[256,256]{1,0:T(8,128)(2,1)S(1)}, bf16[256,256]{1,0:T(8,128)(2,1)S(1)}, u32[]{:S(2)}, u32[]{:S(2)}) collective-permute-start(bf16[256,256]{1,0:T(8,128)(2,1)S(1)} %get-tuple-element.136), channel_id=1, source_target_pairs={{0,1},{1,2},{2,3},{3,0},{4,5},{5,6},{6,7},{7,4},{8,9},{9,10},{10,1... | collective-permute-start | bytes 393224 | tf_op jit(solution)/shard_map/ppermute | solution.py:199
  322.2 33.9 %collective-permute-start.62 = (bf16[256,512]{1,0:T(8,128)(2,1)}, bf16[256,512]{1,0:T(8,128)(2,1)}, u32[]{:S(2)}, u32[]{:S(2)}) collective-permute-start(bf16[256,512]{1,0:T(8,128)(2,1)} %get-tuple-element.103), channel_id=1, source_target_pairs={{0,4},{4,0},{1,5},{5,1},{2,6},{6,2},{3,7},{7,3},{8,12},{12,8},{9,1... | collective-permute-start | bytes 786440 | tf_op jit(solution)/shard_map/ppermute | solution.py:199
  322.3 90.1 %collective-permute-start.72 = (bf16[128,2048]{1,0:T(8,128)(2,1)}, bf16[128,2048]{1,0:T(8,128)(2,1)}, u32[]{:S(2)}, u32[]{:S(2)}) collective-permute-start(bf16[128,2048]{1,0:T(8,128)(2,1)} %select_bitcast_fusion.25), channel_id=1, source_target_pairs={{0,16},{16,0},{1,17},{17,1},{2,18},{18,2},{3,19},{19,3},{4,20},{20... | collective-permute-start | bytes 1572872 | tf_op jit(solution)/shard_map/ppermute | solution.py:199
  353.1 25.3 %collective-permute-start.42 = (bf16[256,768]{1,0:T(8,128)(2,1)S(1)}, bf16[256,768]{1,0:T(8,128)(2,1)S(1)}, u32[]{:S(2)}, u32[]{:S(2)}) collective-permute-start(bf16[256,768]{1,0:T(8,128)(2,1)S(1)} %copy-done.60), channel_id=1, source_target_pairs={{0,3},{1,0},{2,1},{3,2},{4,7},{5,4},{6,5},{7,6},{8,11},{9,8},{10,9... | collective-permute-start | bytes 1179656 | tf_op jit(solution)/shard_map/ppermute | solution.py:199
  356.1 23.4 %collective-permute-start.40 = (bf16[256,768]{1,0:T(8,128)(2,1)S(1)}, bf16[256,768]{1,0:T(8,128)(2,1)S(1)}, u32[]{:S(2)}, u32[]{:S(2)}) collective-permute-start(bf16[256,768]{1,0:T(8,128)(2,1)S(1)} %copy-done.59), channel_id=1, source_target_pairs={{0,1},{1,2},{2,3},{3,0},{4,5},{5,6},{6,7},{7,4},{8,9},{9,10},{10,1... | collective-permute-start | bytes 1179656 | tf_op jit(solution)/shard_map/ppermute | solution.py:199
  361.8 52.9 %collective-permute-start.74 = (bf16[128,2048]{1,0:T(8,128)(2,1)}, bf16[128,2048]{1,0:T(8,128)(2,1)}, u32[]{:S(2)}, u32[]{:S(2)}) collective-permute-start(bf16[128,2048]{1,0:T(8,128)(2,1)} %select_bitcast_fusion.24), channel_id=1, source_target_pairs={{0,8},{8,0},{1,9},{9,1},{2,10},{10,2},{3,11},{11,3},{4,12},{12,4},... | collective-permute-start | bytes 1572872 | tf_op jit(solution)/shard_map/ppermute | solution.py:199
  387.9 37.7 %all-to-all-start.1 = ((f32[32,1,384]{2,1,0:T(1,128)}), f32[32,1,384]{2,1,0:T(1,128)S(1)}, u32[]{:S(2)}, u32[]{:S(2)}) async-start(f32[32,1,384]{2,1,0:T(1,128)} %all_to_all.11), calls=%async_computation.1 | async-start | bytes 98304 | tf_op jit(solution)/shard_map/all_to_all | solution.py:478
  392.6 82.0 %collective-permute-start.52 = (bf16[1024,384]{1,0:T(8,128)(2,1)}, bf16[1024,384]{1,0:T(8,128)(2,1)}, u32[]{:S(2)}, u32[]{:S(2)}) collective-permute-start(bf16[1024,384]{1,0:T(8,128)(2,1)} %convolution_convert_fusion.3), channel_id=1, source_target_pairs={{0,4},{4,0},{1,5},{5,1},{2,6},{6,2},{3,7},{7,3},{8,12},{12,8},{9,1... | collective-permute-start | bytes 2359304 | tf_op jit(solution)/shard_map/ppermute | solution.py:199
  431.0 25.4 %collective-permute-start.76 = (bf16[2,32,2048]{2,1,0:T(8,128)(2,1)}, bf16[2,32,2048]{2,1,0:T(8,128)(2,1)S(1)}, u32[]{:S(2)}, u32[]{:S(2)}) collective-permute-start(bf16[2,32,2048]{2,1,0:T(8,128)(2,1)} %get-tuple-element.101), channel_id=1, source_target_pairs={{0,2},{1,3},{2,0},{3,1},{4,6},{5,7},{6,4},{7,5},{8,10},{9,11},{10,... | collective-permute-start | bytes 786440 | tf_op jit(solution)/shard_map/ppermute | solution.py:199
  433.3 23.2 %collective-permute-start.75 = (bf16[2,32,2048]{2,1,0:T(8,128)(2,1)S(1)}, bf16[2,32,2048]{2,1,0:T(8,128)(2,1)S(1)}, u32[]{:S(2)}, u32[]{:S(2)}) collective-permute-start(bf16[2,32,2048]{2,1,0:T(8,128)(2,1)S(1)} %get-tuple-element.100), channel_id=1, source_target_pairs={{0,1},{1,2},{2,3},{3,0},{4,5},{5,6},{6,7},{7,4},{8,9},{9,10},{10,1... | collective-permute-start | bytes 786440 | tf_op jit(solution)/shard_map/ppermute | solution.py:199
  (162 other events, 2128.1 us)

commit v3 on v2

--- a/solution.py
+++ b/solution.py
@@ -84,7 +84,7 @@
 
 def attend_forward(projected):
     length, width = projected.shape[0], projected.shape[1] // 3
-    block = min(256, length)
+    block = min(512, length)
     heads = width // HD
     return pl.pallas_call(
         functools.partial(forward_kernel, 1.0 / math.sqrt(HD)),
@@ -164,7 +164,7 @@
 
 def attend_backward(projected, outputs, log_total, grad_out):
     length, width = outputs.shape
-    block = min(256, length)
+    block = min(512, length)
     heads = width // HD
     full = pl.BlockSpec((length, width), lambda i, h: (0, 0))
     return pl.pallas_call(
@@ -301,8 +301,9 @@
     def over_plane(full):
         line_rows = full.shape[0] // (ny * nx * nc)
         parts = full.reshape(ny, nx, nc, line_rows, full.shape[1])
-        low = reduce_blocks(parts[:, :, 0], "x", nx, 1).astype(BF16)
-        high = reduce_blocks(parts[:, :, 1], "y", ny, 0).astype(BF16)
+        low = reduce_blocks(parts[:, :, 0], "x", nx, 1)
+        high = reduce_blocks(parts[:, :, 1], "y", ny, 0)
+        low, high = low.astype(BF16), high.astype(BF16)
         low = reduce_blocks(low, "y", ny, 0).astype(BF16)
         high = reduce_blocks(high, "x", nx, 0).astype(BF16)
         return jnp.stack([low, high], 0)
@@ -348,8 +349,11 @@
     plane = gather_blocks(gather_blocks(own_line, "x", nx, 0), "y", ny, 0)
     own_qkv = gather_blocks(plane, "core", nc, 2).reshape(width, 3 * own)
 
+    up_out = own_columns(w_up), own_columns(w_out)
+    up_out = jnp.concatenate(up_out, 2)
+    up_line = shifts(up_out, "seq", ns)
     small = (b_query, b_value, b_out, ln1_gain, ln1_shift, b_up, b_down, ln2_gain, ln2_shift)
-    packed = jnp.concatenate((after(small[0], *came),) + small[1:])[None]
+    packed = jnp.concatenate((after(small[0], *up_line),) + small[1:])[None]
     packed = lax.all_to_all(
         jnp.tile(packed, (devices, 1)), ALL, split_axis=0, concat_axis=0, tiled=True
     ).astype(F32)
@@ -360,9 +364,6 @@
     (bias_query, bias_value, bias_out, gain_one, shift_one, bias_up, bias_down, gain_two,
      shift_two) = vectors
 
-    up_out = own_columns(w_up), own_columns(w_out)
-    up_out = after(jnp.concatenate(up_out, 2), *came)
-    up_line = shifts(up_out, "seq", ns)
     hidden_sent = after(hidden_states, *up_line)
     hidden_line = relayed(hidden_sent, "seq", ns)
     seq_hidden = jnp.concatenate([hidden_sent] + hidden_line, 0)
@@ -474,8 +475,9 @@
     own_sums = jnp.sum(grad_own.astype(F32), 0)
 
     def sum_small(parts):
+        parts = lax.optimization_barrier(tuple(parts) + (grad_tok,))[:-1]
         stacked = jnp.concatenate([part.reshape(devices, -1) for part in parts], 1)
-        arrived = lax.all_to_all(after(stacked, grad_tok), ALL, split_axis=0, concat_axis=0, tiled=True)
+        arrived = lax.all_to_all(stacked, ALL, split_axis=0, concat_axis=0, tiled=True)
         total = jnp.sum(arrived, 0)
         ends, place = [], 0
         for part in parts:

time: 517 us -> 511 us (0.988)
  starting transfers between devices: 144 us -> 130 us
  waiting for transfers between devices: 194 us -> 207 us
  Pallas kernels: 32.1 us -> 24.4 us
    ppermute x81, waiting for transfers between devices: 161 us -> 183 us  [shift(): lax.ppermute(block, axis, [(i, (i + distance) % size) for i in range(size)])]
    ppermute x81, starting transfers between devices: 121 us -> 113 us  [shift(): lax.ppermute(block, axis, [(i, (i + distance) % size) for i in range(size)])]
    ppermute x3, waiting for transfers between devices: 27.3 us -> 21.3 us  [relayed(): lax.ppermute(down[-1], axis, [(i, i - 1) for i in range(1, size - step +...]
    select_n x22 -> x23, other arithmetic: 12.2 us -> 12.7 us  [pick(): return jnp.where(index == 0, first, second)]
    unnamed x200 -> x206, local copies, waits for them, and re-layouts: 11.3 us -> 11 us
  transfers between devices with their start and end apart: 89 -> 89, of which waited for: 33 -> 40; matrix products, arithmetic and copies ran while one was open for 23% -> 24% of each run, Pallas kernels for 6% -> 5%
where the time goes in v3:
time: 511 us; the launch traced here: 501 us
  waiting for transfers between devices  207 us (41%)
  starting transfers between devices  130 us (25%)
  other arithmetic  53.6 us (10%)
  matrix products  42.9 us (8%)
  local copies, waits for them, and re-layouts  39.4 us (8%)
  Pallas kernels  24.4 us (5%)
    ppermute x81, waiting for transfers between devices, shift(): lax.ppermute(block, axis, [(i, (i + distance) % size) for i in range(size)])  183 us
    ppermute x81, starting transfers between devices, shift(): lax.ppermute(block, axis, [(i, (i + distance) % size) for i in range(size)])  113 us
    ppermute x3, waiting for transfers between devices, relayed(): lax.ppermute(down[-1], axis, [(i, i - 1) for i in range(1, size - step +...  21.3 us
    dot_general x6, matrix products, contract_last(): lax.dot_general(left, right, (((1,), (1,)), ((), ())), preferred_element_...  16.6 us
    pallas_call x1, Pallas kernels, attend_backward(): pl.pallas_call(functools.partial(backward_kernel, 1.0 / math.sqrt(HD), bl...  13.6 us
    dot_general x5, matrix products, dot(): return jnp.dot(left, right, preferred_element_type=F32)  13.2 us
    dot_general x5, matrix products, contract_first(): lax.dot_general(left, right, (((0,), (0,)), ((), ())), preferred_element_...  13.2 us
    select_n x23, other arithmetic, pick(): return jnp.where(index == 0, first, second)  12.7 us
  transfers between devices with their start and end apart: 89, of which 40 were waited for; matrix products, arithmetic and copies ran while one was open for 24% of the time, Pallas kernels for 5%

profile of v3, /device:TPU:0, one launch (start us, length us, event | category | flops | bytes accessed | tf_op | source)
XLA Modules:
  0.0 501.2 jit_solution(5405234430232955529)
XLA Ops:
  27.8 19.3 %collective-permute-done.3 = bf16[2,32,2560]{2,1,0:T(8,128)(2,1)S(1)} collective-permute-done((bf16[2,32,2560]{2,1,0:T(8,128)(2,1)S(1)}, bf16[2,32,2560]{2,1,0:T(8,128)(2,1)S(1)}, u32[]{:S(2)}, u32[]{:S(2)}) %collective-permute-start.3) | collective-permute-done | bytes 327712 | tf_op jit(solution)/shard_map/ppermute | solution.py:199
  48.4 5.4 %collective-permute-start.6 = (bf16[256,1024]{1,0:T(8,128)(2,1)}, bf16[256,1024]{1,0:T(8,128)(2,1)}, u32[]{:S(2)}, u32[]{:S(2)}) collective-permute-start(bf16[256,1024]{1,0:T(8,128)(2,1)} %param.15), channel_id=1, source_target_pairs={{0,1},{1,2},{2,3},{4,5},{5,6},{6,7},{8,9},{9,10},{10,11},{12,13},{... | collective-permute-start | bytes 1572872 | tf_op jit(solution)/shard_map/ppermute | solution.py:214
  80.5 8.4 %collective-permute-done.9 = bf16[256,1024]{1,0:T(8,128)(2,1)S(1)} collective-permute-done((bf16[256,1024]{1,0:T(8,128)(2,1)}, bf16[256,1024]{1,0:T(8,128)(2,1)S(1)}, u32[]{:S(2)}, u32[]{:S(2)}) %collective-permute-start.9) | collective-permute-done | bytes 524320 | tf_op jit(solution)/shard_map/ppermute | solution.py:215
  91.2 13.0 %collective-permute-done.10 = bf16[256,1024]{1,0:T(8,128)(2,1)S(1)} collective-permute-done((bf16[256,1024]{1,0:T(8,128)(2,1)S(1)}, bf16[256,1024]{1,0:T(8,128)(2,1)S(1)}, u32[]{:S(2)}, u32[]{:S(2)}) %collective-permute-start.10) | collective-permute-done | bytes 524320 | tf_op jit(solution)/shard_map/ppermute | solution.py:215
  109.2 10.8 %attend_forward.1 = (bf16[1024,256]{1,0:T(8,128)(2,1)S(1)}, f32[4,1024]{1,0:T(4,128)S(1)}) custom-call(bf16[1024,768]{1,0:T(8,128)(2,1)S(1)} %add_convert_fusion.query_ref.key_ref.value_ref, bf16[1024,768]{1,0:T(8,128)(2,1)S(1)} %add_convert_fusion.query_ref.key_ref.value_ref, bf16[1024,768]{1,0:T(8,128)(2,1)S(1)} %add_convert_fusion.query_ref.key_ref.value_ref), custom_call_target="tpu_custom_call" | custom-call | flops 1073741824 | bytes 2097152 | tf_op jit(solution)/shard_map/attend_forward/pallas_call | solution.py:89
  125.4 6.2 %collective-permute-done.18 = bf16[256,256]{1,0:T(8,128)(2,1)S(1)} collective-permute-done((bf16[256,256]{1,0:T(8,128)(2,1)S(1)}, bf16[256,256]{1,0:T(8,128)(2,1)S(1)}, u32[]{:S(2)}, u32[]{:S(2)}) %collective-permute-start.18) | collective-permute-done | bytes 131104 | tf_op jit(solution)/shard_map/ppermute | solution.py:199
  133.4 11.1 %collective-permute-start.27 = (bf16[2,32,2048]{2,1,0:T(8,128)(2,1)S(1)}, bf16[2,32,2048]{2,1,0:T(8,128)(2,1)S(1)}, u32[]{:S(2)}, u32[]{:S(2)}) collective-permute-start(bf16[2,32,2048]{2,1,0:T(8,128)(2,1)S(1)} %pad_maximum_fusion.28), channel_id=1, source_target_pairs={{0,1},{1,2},{2,3},{3,0},{4,5},{5,6},{6,7},{7,4},{8,9},{9,10},{10,1... | collective-permute-start | bytes 786440 | tf_op jit(solution)/shard_map/ppermute | solution.py:199
  145.6 5.7 %collective-permute-done.28 = bf16[2,32,2048]{2,1,0:T(8,128)(2,1)S(1)} collective-permute-done((bf16[2,32,2048]{2,1,0:T(8,128)(2,1)S(1)}, bf16[2,32,2048]{2,1,0:T(8,128)(2,1)S(1)}, u32[]{:S(2)}, u32[]{:S(2)}) %collective-permute-start.28) | collective-permute-done | bytes 262176 | tf_op jit(solution)/shard_map/ppermute | solution.py:199
  153.3 11.0 %collective-permute-start.44 = (bf16[2,32,1536]{2,1,0:T(8,128)(2,1)S(1)}, bf16[2,32,1536]{2,1,0:T(8,128)(2,1)S(1)}, u32[]{:S(2)}, u32[]{:S(2)}) collective-permute-start(bf16[2,32,1536]{2,1,0:T(8,128)(2,1)S(1)} %pad_maximum_fusion.30), channel_id=1, source_target_pairs={{0,1},{1,2},{2,3},{3,0},{4,5},{5,6},{6,7},{7,4},{8,9},{9,10},{10,1... | collective-permute-start | bytes 589832 | tf_op jit(solution)/shard_map/ppermute | solution.py:199
  179.4 8.3 %collective-permute-done.32 = bf16[128,2048]{1,0:T(8,128)(2,1)S(1)} collective-permute-done((bf16[128,2048]{1,0:T(8,128)(2,1)S(1)}, bf16[128,2048]{1,0:T(8,128)(2,1)S(1)}, u32[]{:S(2)}, u32[]{:S(2)}) %collective-permute-start.32) | collective-permute-done | bytes 524320 | tf_op jit(solution)/shard_map/ppermute | solution.py:199
  191.1 18.1 %collective-permute-done.31 = bf16[2,128,2048]{2,1,0:T(8,128)(2,1)S(1)} collective-permute-done((bf16[2,128,2048]{2,1,0:T(8,128)(2,1)S(1)}, bf16[2,128,2048]{2,1,0:T(8,128)(2,1)S(1)}, u32[]{:S(2)}, u32[]{:S(2)}) %collective-permute-start.31) | collective-permute-done | bytes 1048608 | tf_op jit(solution)/shard_map/ppermute | solution.py:199
  233.4 11.1 %collective-permute-done.50 = bf16[2,128,1536]{2,1,0:T(8,128)(2,1)S(1)} collective-permute-done((bf16[2,128,1536]{2,1,0:T(8,128)(2,1)S(1)}, bf16[2,128,1536]{2,1,0:T(8,128)(2,1)S(1)}, u32[]{:S(2)}, u32[]{:S(2)}) %collective-permute-start.50) | collective-permute-done | bytes 786464 | tf_op jit(solution)/shard_map/ppermute | solution.py:199
  251.0 5.4 %fusion.152 = (f32[2048]{0:T(1024)S(1)}, bf16[512,2048]{1,0:T(8,128)(2,1)S(1)}) fusion(f32[512,2048]{1,0:T(8,128)S(1)} %copy-done.97, f32[2048]{0:T(1024)S(1)} %copy-done.83, bf16[1024,2048]{1,0:T(8,128)(2,1)S(1)} %bitcast.523, bf16[256,1024]{1,0:T(8,128)(2,1)S(1)} %collective-permute-done.35, bf16[256,1024]{1,0:T(8,128)(2,1)S(1)} %convert_element_type.331), kind=kOutput, calls=%fused_computation.404 | convolution fusion | flops 2162161664 | bytes 11550720 | tf_op jit(solution)/shard_map/dot_general | solution.py:46
  282.1 6.6 %collective-permute-done.71 = bf16[2,128,2048]{2,1,0:T(8,128)(2,1)} collective-permute-done((bf16[2,128,2048]{2,1,0:T(8,128)(2,1)}, bf16[2,128,2048]{2,1,0:T(8,128)(2,1)}, u32[]{:S(2)}, u32[]{:S(2)}) %collective-permute-start.71) | collective-permute-done | bytes 1048608 | tf_op jit(solution)/shard_map/ppermute | solution.py:199
  293.7 19.4 %collective-permute-done.81 = bf16[2,128,2048]{2,1,0:T(8,128)(2,1)} collective-permute-done((bf16[2,128,2048]{2,1,0:T(8,128)(2,1)}, bf16[2,128,2048]{2,1,0:T(8,128)(2,1)}, u32[]{:S(2)}, u32[]{:S(2)}) %collective-permute-start.81) | collective-permute-done | bytes 1048608 | tf_op jit(solution)/shard_map/ppermute | solution.py:199
  322.1 13.6 %attend_backward.1 = bf16[1024,768]{1,0:T(8,128)(2,1)S(1)} custom-call(bf16[1024,768]{1,0:T(8,128)(2,1)S(1)} %copy-done.1, bf16[1024,768]{1,0:T(8,128)(2,1)S(1)} %copy-done.1, bf16[1024,768]{1,0:T(8,128)(2,1)S(1)} %copy-done.1, bf16[1024,256]{1,0:T(8,128)(2,1)S(1)} %get-tuple-element.34.out_ref, f32[4,1024]{1,0:T(4,128)S(1)} %get-tuple-element.36.total_ref, ...), custom_call_target="tpu_custom_call" | custom-call | flops 2684354560 | bytes 4194304 | tf_op jit(solution)/shard_map/attend_backward/pallas_call | solution.py:170
  359.9 13.5 %collective-permute-done.42 = bf16[256,768]{1,0:T(8,128)(2,1)S(1)} collective-permute-done((bf16[256,768]{1,0:T(8,128)(2,1)S(1)}, bf16[256,768]{1,0:T(8,128)(2,1)S(1)}, u32[]{:S(2)}, u32[]{:S(2)}) %collective-permute-start.42) | collective-permute-done | bytes 393248 | tf_op jit(solution)/shard_map/ppermute | solution.py:199
  398.0 7.1 %collective-permute-done.65 = bf16[2,128,512]{2,1,0:T(8,128)(2,1)S(1)} collective-permute-done((bf16[2,128,512]{2,1,0:T(8,128)(2,1)S(1)}, bf16[2,128,512]{2,1,0:T(8,128)(2,1)S(1)}, u32[]{:S(2)}, u32[]{:S(2)}) %collective-permute-start.65) | collective-permute-done | bytes 262176 | tf_op jit(solution)/shard_map/ppermute | solution.py:199
  411.7 6.2 %collective-permute-start.69 = (bf16[2,32,512]{2,1,0:T(8,128)(2,1)}, bf16[2,32,512]{2,1,0:T(8,128)(2,1)}, u32[]{:S(2)}, u32[]{:S(2)}) collective-permute-start(bf16[2,32,512]{2,1,0:T(8,128)(2,1)} %get-tuple-element.177), channel_id=1, source_target_pairs={{0,3},{1,0},{2,1},{3,2},{4,7},{5,4},{6,5},{7,6},{8,11},{9,8},{10,9... | collective-permute-start | bytes 196616 | tf_op jit(solution)/shard_map/ppermute | solution.py:199
  427.0 10.3 %collective-permute-start.75 = (bf16[2,32,2048]{2,1,0:T(8,128)(2,1)S(1)}, bf16[2,32,2048]{2,1,0:T(8,128)(2,1)S(1)}, u32[]{:S(2)}, u32[]{:S(2)}) collective-permute-start(bf16[2,32,2048]{2,1,0:T(8,128)(2,1)S(1)} %get-tuple-element.113), channel_id=1, source_target_pairs={{0,1},{1,2},{2,3},{3,0},{4,5},{5,6},{6,7},{7,4},{8,9},{9,10},{10,1... | collective-permute-start | bytes 786440 | tf_op jit(solution)/shard_map/ppermute | solution.py:199
  438.0 12.2 %collective-permute-done.76 = bf16[2,32,2048]{2,1,0:T(8,128)(2,1)S(1)} collective-permute-done((bf16[2,32,2048]{2,1,0:T(8,128)(2,1)}, bf16[2,32,2048]{2,1,0:T(8,128)(2,1)S(1)}, u32[]{:S(2)}, u32[]{:S(2)}) %collective-permute-start.76) | collective-permute-done | bytes 262176 | tf_op jit(solution)/shard_map/ppermute | solution.py:199
  450.3 7.6 %collective-permute-start.83 = (bf16[2,32,2048]{2,1,0:T(8,128)(2,1)S(1)}, bf16[2,32,2048]{2,1,0:T(8,128)(2,1)S(1)}, u32[]{:S(2)}, u32[]{:S(2)}) collective-permute-start(bf16[2,32,2048]{2,1,0:T(8,128)(2,1)S(1)} %get-tuple-element.110), channel_id=1, source_target_pairs={{0,1},{1,2},{2,3},{3,0},{4,5},{5,6},{6,7},{7,4},{8,9},{9,10},{10,1... | collective-permute-start | bytes 786440 | tf_op jit(solution)/shard_map/ppermute | solution.py:199
  458.2 9.9 %collective-permute-done.84 = bf16[2,32,2048]{2,1,0:T(8,128)(2,1)S(1)} collective-permute-done((bf16[2,32,2048]{2,1,0:T(8,128)(2,1)S(1)}, bf16[2,32,2048]{2,1,0:T(8,128)(2,1)S(1)}, u32[]{:S(2)}, u32[]{:S(2)}) %collective-permute-start.84) | collective-permute-done | bytes 262176 | tf_op jit(solution)/shard_map/ppermute | solution.py:199
  473.3 5.2 %collective-permute-done.55 = bf16[2,128,384]{2,1,0:T(8,128)(2,1)S(1)} collective-permute-done((bf16[2,128,384]{2,1,0:T(8,128)(2,1)S(1)}, bf16[2,128,384]{2,1,0:T(8,128)(2,1)S(1)}, u32[]{:S(2)}, u32[]{:S(2)}) %collective-permute-start.55) | collective-permute-done | bytes 196640 | tf_op jit(solution)/shard_map/ppermute | solution.py:199
  (587 shorter events, 252.4 us)
Async XLA Ops:
  19.6 27.5 %collective-permute-start.3 = (bf16[2,32,2560]{2,1,0:T(8,128)(2,1)S(1)}, bf16[2,32,2560]{2,1,0:T(8,128)(2,1)S(1)}, u32[]{:S(2)}, u32[]{:S(2)}) collective-permute-start(bf16[2,32,2560]{2,1,0:T(8,128)(2,1)S(1)} %maximum_maximum_fusion), channel_id=1, source_target_pairs={{0,2},{1,3},{2,0},{3,1},{4,6},{5,7},{6,4},{7,5},{8,10},{9,11},{10,... | collective-permute-start | bytes 983048 | tf_op jit(solution)/shard_map/ppermute | solution.py:199
  19.7 27.5 %collective-permute-start.4 = (bf16[2,32,2560]{2,1,0:T(8,128)(2,1)S(1)}, bf16[2,32,2560]{2,1,0:T(8,128)(2,1)S(1)}, u32[]{:S(2)}, u32[]{:S(2)}) collective-permute-start(bf16[2,32,2560]{2,1,0:T(8,128)(2,1)S(1)} %maximum_maximum_fusion), channel_id=1, source_target_pairs={{0,1},{1,2},{2,3},{3,0},{4,5},{5,6},{6,7},{7,4},{8,9},{9,10},{10,1... | collective-permute-start | bytes 983048 | tf_op jit(solution)/shard_map/ppermute | solution.py:199
  21.3 49.9 %collective-permute-start.15 = (bf16[2,128,768]{2,1,0:T(8,128)(2,1)S(1)}, bf16[2,128,768]{2,1,0:T(8,128)(2,1)}, u32[]{:S(2)}, u32[]{:S(2)}) collective-permute-start(bf16[2,128,768]{2,1,0:T(8,128)(2,1)S(1)} %pad_maximum_fusion.27), channel_id=1, source_target_pairs={{0,16},{16,0},{1,17},{17,1},{2,18},{18,2},{3,19},{19,3},{4,20},{20... | collective-permute-start | bytes 1179656 | tf_op jit(solution)/shard_map/ppermute | solution.py:199
  47.1 25.3 %collective-permute-start.5 = (bf16[256,1024]{1,0:T(8,128)(2,1)}, bf16[256,1024]{1,0:T(8,128)(2,1)}, u32[]{:S(2)}, u32[]{:S(2)}) collective-permute-start(bf16[256,1024]{1,0:T(8,128)(2,1)} %param.15), channel_id=1, source_target_pairs={{1,0},{2,1},{3,2},{5,4},{6,5},{7,6},{9,8},{10,9},{11,10},{13,12},{... | collective-permute-start | bytes 1572872 | tf_op jit(solution)/shard_map/ppermute | solution.py:215
  48.4 25.3 %collective-permute-start.6 = (bf16[256,1024]{1,0:T(8,128)(2,1)}, bf16[256,1024]{1,0:T(8,128)(2,1)}, u32[]{:S(2)}, u32[]{:S(2)}) collective-permute-start(bf16[256,1024]{1,0:T(8,128)(2,1)} %param.15), channel_id=1, source_target_pairs={{0,1},{1,2},{2,3},{4,5},{5,6},{6,7},{8,9},{9,10},{10,11},{12,13},{... | collective-permute-start | bytes 1572872 | tf_op jit(solution)/shard_map/ppermute | solution.py:214
  78.7 95.1 %collective-permute-start.21 = (bf16[2,128,2560]{2,1,0:T(8,128)(2,1)S(1)}, bf16[2,128,2560]{2,1,0:T(8,128)(2,1)S(1)}, u32[]{:S(2)}, u32[]{:S(2)}) collective-permute-start(bf16[2,128,2560]{2,1,0:T(8,128)(2,1)S(1)} %pad_maximum_fusion.7), channel_id=1, source_target_pairs={{0,16},{16,0},{1,17},{17,1},{2,18},{18,2},{3,19},{19,3},{4,20},{20... | collective-permute-start | bytes 3932168 | tf_op jit(solution)/shard_map/ppermute | solution.py:199
  124.1 49.9 %collective-permute-start.23 = (bf16[2,128,2560]{2,1,0:T(8,128)(2,1)S(1)}, bf16[2,128,2560]{2,1,0:T(8,128)(2,1)S(1)}, u32[]{:S(2)}, u32[]{:S(2)}) collective-permute-start(bf16[2,128,2560]{2,1,0:T(8,128)(2,1)S(1)} %pad_maximum_fusion.8), channel_id=1, source_target_pairs={{0,8},{8,0},{1,9},{9,1},{2,10},{10,2},{3,11},{11,3},{4,12},{12,4},... | collective-permute-start | bytes 3932168 | tf_op jit(solution)/shard_map/ppermute | solution.py:199
  178.7 30.5 %collective-permute-start.31 = (bf16[2,128,2048]{2,1,0:T(8,128)(2,1)S(1)}, bf16[2,128,2048]{2,1,0:T(8,128)(2,1)S(1)}, u32[]{:S(2)}, u32[]{:S(2)}) collective-permute-start(bf16[2,128,2048]{2,1,0:T(8,128)(2,1)S(1)} %pad_maximum_fusion.11), channel_id=1, source_target_pairs={{0,16},{16,0},{1,17},{17,1},{2,18},{18,2},{3,19},{19,3},{4,20},{20... | collective-permute-start | bytes 3145736 | tf_op jit(solution)/shard_map/ppermute | solution.py:199
  187.9 23.3 %collective-permute-start.33 = (bf16[2,128,2048]{2,1,0:T(8,128)(2,1)S(1)}, bf16[2,128,2048]{2,1,0:T(8,128)(2,1)S(1)}, u32[]{:S(2)}, u32[]{:S(2)}) collective-permute-start(bf16[2,128,2048]{2,1,0:T(8,128)(2,1)S(1)} %pad_maximum_fusion.12), channel_id=1, source_target_pairs={{0,8},{8,0},{1,9},{9,1},{2,10},{10,2},{3,11},{11,3},{4,12},{12,4},... | collective-permute-start | bytes 3145736 | tf_op jit(solution)/shard_map/ppermute | solution.py:199
  223.0 124.4 %collective-permute-start.61 = (bf16[256,1024]{1,0:T(8,128)(2,1)}, bf16[256,1024]{1,0:T(8,128)(2,1)}, u32[]{:S(2)}, u32[]{:S(2)}) collective-permute-start(bf16[256,1024]{1,0:T(8,128)(2,1)} %pad_maximum_fusion.23), channel_id=1, source_target_pairs={{0,4},{4,0},{1,5},{5,1},{2,6},{6,2},{3,7},{7,3},{8,12},{12,8},{9,1... | collective-permute-start | bytes 1572872 | tf_op jit(solution)/shard_map/ppermute | solution.py:199
  248.5 248.1 %collective-permute-start.51 = (bf16[1024,1536]{1,0:T(8,128)(2,1)}, bf16[1024,1536]{1,0:T(8,128)(2,1)}, u32[]{:S(2)}, u32[]{:S(2)}) collective-permute-start(bf16[1024,1536]{1,0:T(8,128)(2,1)} %bitcast.87), channel_id=1, source_target_pairs={{0,4},{4,0},{1,5},{5,1},{2,6},{6,2},{3,7},{7,3},{8,12},{12,8},{9,1... | collective-permute-start | bytes 9437192 | tf_op jit(solution)/shard_map/ppermute | solution.py:199
  263.7 25.0 %collective-permute-start.71 = (bf16[2,128,2048]{2,1,0:T(8,128)(2,1)}, bf16[2,128,2048]{2,1,0:T(8,128)(2,1)}, u32[]{:S(2)}, u32[]{:S(2)}) collective-permute-start(bf16[2,128,2048]{2,1,0:T(8,128)(2,1)} %select_bitcast_fusion.7), channel_id=1, source_target_pairs={{0,8},{8,0},{1,9},{9,1},{2,10},{10,2},{3,11},{11,3},{4,12},{12,4},... | collective-permute-start | bytes 3145736 | tf_op jit(solution)/shard_map/ppermute | solution.py:199
  265.6 26.6 %collective-permute-start.73 = (bf16[2,128,2048]{2,1,0:T(8,128)(2,1)}, bf16[2,128,2048]{2,1,0:T(8,128)(2,1)S(1)}, u32[]{:S(2)}, u32[]{:S(2)}) collective-permute-start(bf16[2,128,2048]{2,1,0:T(8,128)(2,1)} %select_bitcast_fusion.6), channel_id=1, source_target_pairs={{0,16},{16,0},{1,17},{17,1},{2,18},{18,2},{3,19},{19,3},{4,20},{20... | collective-permute-start | bytes 3145736 | tf_op jit(solution)/shard_map/ppermute | solution.py:199
  272.9 40.2 %collective-permute-start.81 = (bf16[2,128,2048]{2,1,0:T(8,128)(2,1)}, bf16[2,128,2048]{2,1,0:T(8,128)(2,1)}, u32[]{:S(2)}, u32[]{:S(2)}) collective-permute-start(bf16[2,128,2048]{2,1,0:T(8,128)(2,1)} %select_bitcast_fusion.4), channel_id=1, source_target_pairs={{0,16},{16,0},{1,17},{17,1},{2,18},{18,2},{3,19},{19,3},{4,20},{20... | collective-permute-start | bytes 3145736 | tf_op jit(solution)/shard_map/ppermute | solution.py:199
  288.8 27.2 %collective-permute-start.79 = (bf16[2,128,2048]{2,1,0:T(8,128)(2,1)S(1)}, bf16[2,128,2048]{2,1,0:T(8,128)(2,1)S(1)}, u32[]{:S(2)}, u32[]{:S(2)}) collective-permute-start(bf16[2,128,2048]{2,1,0:T(8,128)(2,1)S(1)} %copy-done.37), channel_id=1, source_target_pairs={{0,8},{8,0},{1,9},{9,1},{2,10},{10,2},{3,11},{11,3},{4,12},{12,4},... | collective-permute-start | bytes 3145736 | tf_op jit(solution)/shard_map/ppermute | solution.py:199
  292.2 26.8 %collective-permute-start.39 = (bf16[256,256]{1,0:T(8,128)(2,1)S(1)}, bf16[256,256]{1,0:T(8,128)(2,1)S(1)}, u32[]{:S(2)}, u32[]{:S(2)}) collective-permute-start(bf16[256,256]{1,0:T(8,128)(2,1)S(1)} %get-tuple-element.149), channel_id=1, source_target_pairs={{0,1},{1,2},{2,3},{3,0},{4,5},{5,6},{6,7},{7,4},{8,9},{9,10},{10,1... | collective-permute-start | bytes 393224 | tf_op jit(solution)/shard_map/ppermute | solution.py:199
  319.0 30.8 %collective-permute-start.62 = (bf16[256,512]{1,0:T(8,128)(2,1)}, bf16[256,512]{1,0:T(8,128)(2,1)}, u32[]{:S(2)}, u32[]{:S(2)}) collective-permute-start(bf16[256,512]{1,0:T(8,128)(2,1)} %get-tuple-element.116), channel_id=1, source_target_pairs={{0,4},{4,0},{1,5},{5,1},{2,6},{6,2},{3,7},{7,3},{8,12},{12,8},{9,1... | collective-permute-start | bytes 786440 | tf_op jit(solution)/shard_map/ppermute | solution.py:199
  320.7 85.3 %collective-permute-start.72 = (bf16[128,2048]{1,0:T(8,128)(2,1)}, bf16[128,2048]{1,0:T(8,128)(2,1)}, u32[]{:S(2)}, u32[]{:S(2)}) collective-permute-start(bf16[128,2048]{1,0:T(8,128)(2,1)} %select_bitcast_fusion.25), channel_id=1, source_target_pairs={{0,16},{16,0},{1,17},{17,1},{2,18},{18,2},{3,19},{19,3},{4,20},{20... | collective-permute-start | bytes 1572872 | tf_op jit(solution)/shard_map/ppermute | solution.py:199
  348.0 25.5 %collective-permute-start.42 = (bf16[256,768]{1,0:T(8,128)(2,1)S(1)}, bf16[256,768]{1,0:T(8,128)(2,1)S(1)}, u32[]{:S(2)}, u32[]{:S(2)}) collective-permute-start(bf16[256,768]{1,0:T(8,128)(2,1)S(1)} %copy-done.57), channel_id=1, source_target_pairs={{0,3},{1,0},{2,1},{3,2},{4,7},{5,4},{6,5},{7,6},{8,11},{9,8},{10,9... | collective-permute-start | bytes 1179656 | tf_op jit(solution)/shard_map/ppermute | solution.py:199
  349.8 24.4 %collective-permute-start.40 = (bf16[256,768]{1,0:T(8,128)(2,1)S(1)}, bf16[256,768]{1,0:T(8,128)(2,1)S(1)}, u32[]{:S(2)}, u32[]{:S(2)}) collective-permute-start(bf16[256,768]{1,0:T(8,128)(2,1)S(1)} %copy-done.56), channel_id=1, source_target_pairs={{0,1},{1,2},{2,3},{3,0},{4,5},{5,6},{6,7},{7,4},{8,9},{9,10},{10,1... | collective-permute-start | bytes 1179656 | tf_op jit(solution)/shard_map/ppermute | solution.py:199
  358.7 49.8 %collective-permute-start.74 = (bf16[128,2048]{1,0:T(8,128)(2,1)}, bf16[128,2048]{1,0:T(8,128)(2,1)}, u32[]{:S(2)}, u32[]{:S(2)}) collective-permute-start(bf16[128,2048]{1,0:T(8,128)(2,1)} %select_bitcast_fusion.24), channel_id=1, source_target_pairs={{0,8},{8,0},{1,9},{9,1},{2,10},{10,2},{3,11},{11,3},{4,12},{12,4},... | collective-permute-start | bytes 1572872 | tf_op jit(solution)/shard_map/ppermute | solution.py:199
  381.8 37.5 %all-to-all-start.1 = ((f32[32,1,384]{2,1,0:T(1,128)}), f32[32,1,384]{2,1,0:T(1,128)S(1)}, u32[]{:S(2)}, u32[]{:S(2)}) async-start(f32[32,1,384]{2,1,0:T(1,128)} %all_to_all.11), calls=%async_computation.1 | async-start | bytes 98304 | tf_op jit(solution)/shard_map/all_to_all | solution.py:480
  387.1 81.3 %collective-permute-start.52 = (bf16[1024,384]{1,0:T(8,128)(2,1)}, bf16[1024,384]{1,0:T(8,128)(2,1)}, u32[]{:S(2)}, u32[]{:S(2)}) collective-permute-start(bf16[1024,384]{1,0:T(8,128)(2,1)} %convolution_convert_fusion.3), channel_id=1, source_target_pairs={{0,4},{4,0},{1,5},{5,1},{2,6},{6,2},{3,7},{7,3},{8,12},{12,8},{9,1... | collective-permute-start | bytes 2359304 | tf_op jit(solution)/shard_map/ppermute | solution.py:199
  424.8 25.5 %collective-permute-start.76 = (bf16[2,32,2048]{2,1,0:T(8,128)(2,1)}, bf16[2,32,2048]{2,1,0:T(8,128)(2,1)S(1)}, u32[]{:S(2)}, u32[]{:S(2)}) collective-permute-start(bf16[2,32,2048]{2,1,0:T(8,128)(2,1)} %get-tuple-element.114), channel_id=1, source_target_pairs={{0,2},{1,3},{2,0},{3,1},{4,6},{5,7},{6,4},{7,5},{8,10},{9,11},{10,... | collective-permute-start | bytes 786440 | tf_op jit(solution)/shard_map/ppermute | solution.py:199
  (165 other events, 1847.2 us)
